TPU v7x, 256 devices: a whole 4x4x8 slice. The times are simulated.
256 devices in a mesh: dir: 8 (over z_lo, core), box: 32 (over z_hi, x, y).
Axes of the slice: x: 4, y: 4, z: 8 (z_hi: 2, z_lo: 4; z = z_hi * 4 + z_lo), core: 2. Of those that a mesh axis runs over, the one named last changes fastest.
Arguments:
- pattern: bfloat16 [64, 128, 256, 128], P('dir', 'box'), may hold values from -6 to 6
- tap_theta: int32 [64, 12], replicated, may hold values from 0 to 31, as said below
- tap_phi: int32 [128, 12], replicated, may hold values from 0 to 63, as said below
- weight_theta: bfloat16 [64, 12], replicated, may hold values from -1.75 to 1.75
- weight_phi: bfloat16 [128, 12], replicated, may hold values from -1.75 to 1.75
- row_box: int32 [524288], P(('dir', 'box')), may hold values from 0 to 2047, as said below
- row_offset: bfloat16 [3, 524288], P(None, ('dir', 'box')), may hold values from -0.5 to 0.5
- row_fwd: bfloat16 [524288, 128], P(('dir', 'box')), may hold values from -6 to 6
Outputs:
- row_field: bfloat16 [524288, 128], P(('dir', 'box'))
- gradient: float32 [524288], P(('dir', 'box'))
Inputs may be any that keep to these rules, and one draw needn't show every extreme that they name: `tap_theta`: row T holds 12 consecutive increasing indices of the child theta samples. `tap_phi`: row P holds 12 consecutive indices of the child phi samples, taken modulo 64. Device i of the dir+box layout holds rows whose parent box row_box // 8 satisfies parent // 32 == i // 32. From one device at most 256 rows name parent boxes with one remainder modulo 32. In each dir group one remainder, drawn from the seed, is named by exactly 256 rows of every device of the group; a device's other rows are spread over the other remainders as evenly as possible. Octants are arbitrary.
All inputs are finite; a program needn't handle non-finite values.
Results may differ from a plain program's by a relative error of at most 0.0065.
Values may be sent and summed in bfloat16 or wider, within the bound.
A program may use at most 64 MiB of HBM per device.

v0:
```python
import math

import jax
import jax.numpy as jnp
from jax import lax
from jax.sharding import PartitionSpec as P

NT_F = 32
NP_F = 64


box_phase = 50.265482


def spread(taps, weights, count):
    grid = jnp.arange(count, dtype=jnp.int32)
    hit = taps[None, :, :] == grid[:, None, None]
    picked = jnp.where(hit, weights[None, :, :].astype(jnp.float32), jnp.float32(0.0))
    return jnp.sum(picked, axis=2).astype(jnp.bfloat16)


def directions(n_theta, n_phi):
    theta = (jnp.arange(n_theta, dtype=jnp.float32) + 0.5) * (math.pi / n_theta)
    angle_phi = jnp.arange(n_phi, dtype=jnp.float32) * (2.0 * math.pi / n_phi)
    sin_t = jnp.repeat(jnp.sin(theta), n_phi)
    cos_t = jnp.repeat(jnp.cos(theta), n_phi)
    phi_all = jnp.tile(angle_phi, n_theta)
    quad = sin_t * math.sqrt(2.0 / (n_theta * n_phi))
    return (sin_t * jnp.cos(phi_all), sin_t * jnp.sin(phi_all), cos_t, quad)


def positions(offset, octant):
    bits = jnp.stack([octant % 2, octant // 2 % 2, octant // 4], axis=1)
    signs = (2 * bits - 1).astype(jnp.float32)
    return box_phase * (signs * 0.25 + offset.astype(jnp.float32) * 0.5)


def field_rows(pos, stacked, kx, ky, kz, quad):
    angle = pos[:, 0:1] * kx[None, :] + pos[:, 1:2] * ky[None, :] + pos[:, 2:3] * kz[None, :]
    cos_w = (quad[None, :] * jnp.cos(angle)).astype(jnp.bfloat16)
    sin_w = (quad[None, :] * jnp.sin(angle)).astype(jnp.bfloat16)
    phase = jnp.concatenate([cos_w, sin_w], axis=1)
    return jnp.dot(phase, stacked, preferred_element_type=jnp.float32)


def block_rows(count):
    size = min(count, 512)
    while count % size:
        size = size - 1
    return size


def per_device(pattern, tap_theta, tap_phi, weight_theta, weight_phi, row_box, row_offset, row_fwd):
    a_theta = spread(tap_theta, weight_theta, NT_F)
    a_phi = spread(tap_phi, weight_phi, NP_F)
    gathered = lax.all_to_all(
        lax.all_to_all(pattern, "dir", split_axis=2, concat_axis=0, tiled=True),
        "box",
        split_axis=2,
        concat_axis=1,
        tiled=True,
    )[:, :, 0, :]
    whole = jnp.einsum("tT,TPc->tPc", a_theta, gathered, preferred_element_type=jnp.float32).astype(
        jnp.bfloat16
    )
    child = jnp.einsum("pP,tPc->tpc", a_phi, whole, preferred_element_type=jnp.float32).astype(
        jnp.bfloat16
    )
    chans = child.shape[2]
    half = chans // 2
    flat = child.reshape(NT_F * NP_F, chans)
    stacked = jnp.concatenate(
        [flat, jnp.concatenate([-flat[:, half:], flat[:, :half]], axis=1)], axis=0
    )
    kx, ky, kz, quad = directions(NT_F, NP_F)
    owners = lax.axis_size("box")
    rows_dev = row_fwd.shape[0]
    capacity = 4 * rows_dev // owners
    parent = row_box // 8
    octant = row_box % 8
    dest = parent % owners
    onehot = (dest[:, None] == jnp.arange(owners, dtype=jnp.int32)[None, :]).astype(jnp.int32)
    slot = jnp.sum((jnp.cumsum(onehot, axis=0) - onehot) * onehot, axis=1)
    geometry = jnp.concatenate([row_offset.T, octant.astype(jnp.bfloat16)[:, None]], axis=1)
    outgoing = jnp.zeros((owners, capacity, 4), jnp.bfloat16).at[dest, slot].set(geometry)
    incoming = lax.all_to_all(outgoing, "box", split_axis=0, concat_axis=0, tiled=True)
    sources = incoming.shape[0]
    items = incoming.shape[1]
    count = sources * items
    flat_in = incoming.reshape(count, 4)
    where_pos = positions(flat_in[:, :3], flat_in[:, 3].astype(jnp.int32))
    size = block_rows(count)
    pieces = where_pos.reshape(count // size, size, 3)

    def one_piece(piece):
        return field_rows(piece, stacked, kx, ky, kz, quad).astype(jnp.bfloat16)

    fields = lax.map(one_piece, pieces).reshape(sources, items, chans)
    returned = lax.all_to_all(fields, "box", split_axis=0, concat_axis=0, tiled=True)
    row_field = returned[dest, slot]
    gradient = jnp.sum(row_fwd.astype(jnp.float32) * row_field.astype(jnp.float32), axis=1) * (
        0.5 / math.sqrt(chans)
    )
    return (row_field, gradient)


def solution(mesh):
    in_specs = (
        P("dir", "box", None, None),
        P(),
        P(),
        P(),
        P(),
        P(("dir", "box")),
        P(None, ("dir", "box")),
        P(("dir", "box"), None),
    )
    out_specs = (P(("dir", "box"), None), P(("dir", "box")))
    return jax.shard_map(
        per_device, mesh=mesh, in_specs=in_specs, out_specs=out_specs, check_vma=False
    )
```

profile of v0, /device:TPU:1, one launch (start us, length us, event | category | flops | bytes accessed | tf_op | source)
XLA Modules:
  0.0 490.3 jit_solution(14645728561312647927)
XLA Ops:
  12.5 9.1 %reduce-window.6 = s32[32,16,128]{2,1,0:T(8,128)S(1)} reduce-window(s32[32,16,128]{2,1,0:T(8,128)S(1)} %fusion.28, s32[]{:T(128)} %copy.89), window={size=1x1x128 pad=0_0x0_0x127_0}, to_apply=%region_0.1 | reduce-window | flops 8323072 | bytes 524292 | tf_op jit(solution)/shard_map/reduce-window
  33.2 27.3 %all-to-all-done.1 = bf16[8,4,256,128]{3,0,1,2:T(8,128)(2,1)S(1)} async-done(((bf16[8,4,256,128]{3,0,1,2:T(8,128)(2,1)}), bf16[8,4,256,128]{3,0,1,2:T(8,128)(2,1)S(1)}, u32[]{:S(2)}, u32[]{:S(2)}) %all-to-all-start.1) | async-done | bytes 2097184 | tf_op jit(solution)/shard_map/all_to_all | solution.py:57
  60.5 11.3 %all-to-all-start = ((bf16[32,256,4]{1,2,0:T(4,128)(2,1)}), bf16[32,256,4]{1,2,0:T(4,128)(2,1)S(1)}, u32[]{:S(2)}, u32[]{:S(2)}) async-start(bf16[32,256,4]{1,2,0:T(4,128)(2,1)} %copy.67), calls=%async_computation | async-start | bytes 131072 | tf_op jit(solution)/shard_map/all_to_all | solution.py:86
  75.2 7.7 %all-to-all-done = bf16[32,256,4]{1,2,0:T(4,128)(2,1)S(1)} async-done(((bf16[32,256,4]{1,2,0:T(4,128)(2,1)}), bf16[32,256,4]{1,2,0:T(4,128)(2,1)S(1)}, u32[]{:S(2)}, u32[]{:S(2)}) %all-to-all-start) | async-done | bytes 65568 | tf_op jit(solution)/shard_map/all_to_all | solution.py:86
  87.8 47.8 %all-to-all-done.2 = bf16[64,4,32,128]{3,1,0,2:T(4,128)(2,1)S(1)} async-done(((bf16[64,4,32,128]{3,1,0,2:T(4,128)(2,1)}), bf16[64,4,32,128]{3,1,0,2:T(4,128)(2,1)S(1)}, u32[]{:S(2)}, u32[]{:S(2)}) %all-to-all-start.2) | async-done | bytes 2097184 | tf_op jit(solution)/shard_map/all_to_all | solution.py:56
  138.7 289.6 %while.13 = (s32[]{:T(128)}, bf16[16,512,128]{2,1,0:T(8,128)(2,1)S(1)}, f32[16,512,3]{1,2,0:T(4,128)S(1)}, bf16[4096,128]{1,0:T(8,128)(2,1)S(1)}, f32[32]{0:T(12...) while((s32[]{:T(128)}, ...), condition=%wide.region_7.8_spmd.clone.clone.clone, body=%wide.region_6.7_spmd.clone.clone.clone.sunk | while | flops 554766336 | bytes 9731053 | solution.py:98
  139.2 16.2 %multiply_convert_fusion.3 = (bf16[512,2048]{1,0:T(8,128)(2,1)S(1)}, bf16[512,2048]{1,0:T(8,128)(2,1)S(1)}) fusion(f32[2048]{0:T(1024)S(1)} %mul.357, f32[512]{0:T(512)S(1)} %bitcast.84, f32[2048]{0:T(1024)S(1)} %mul.358, f32[512]{0:T(512)S(1)} %bitcast.85, f32[2048]{0:T(1024)S(1)} %mul.359, f32[512]{0:T(512)S(1)} %bitcast.83, f32[2048]{0:T(1024)S(1)} %mul.360), kind=kLoop, calls=%fused_computation.11.clone.1 | loop fusion | flops 9437184 | bytes 4233216 | tf_op jit(solution)/shard_map/while/body/eval_jaxpr/convert_element_type | solution.py:40
  157.3 16.2 %multiply_convert_fusion.3 = (bf16[512,2048]{1,0:T(8,128)(2,1)S(1)}, bf16[512,2048]{1,0:T(8,128)(2,1)S(1)}) fusion(f32[2048]{0:T(1024)S(1)} %mul.357, f32[512]{0:T(512)S(1)} %bitcast.84, f32[2048]{0:T(1024)S(1)} %mul.358, f32[512]{0:T(512)S(1)} %bitcast.85, f32[2048]{0:T(1024)S(1)} %mul.359, f32[512]{0:T(512)S(1)} %bitcast.83, f32[2048]{0:T(1024)S(1)} %mul.360), kind=kLoop, calls=%fused_computation.11.clone.1 | loop fusion | flops 9437184 | bytes 4233216 | tf_op jit(solution)/shard_map/while/body/eval_jaxpr/convert_element_type | solution.py:40
  175.4 16.2 %multiply_convert_fusion.3 = (bf16[512,2048]{1,0:T(8,128)(2,1)S(1)}, bf16[512,2048]{1,0:T(8,128)(2,1)S(1)}) fusion(f32[2048]{0:T(1024)S(1)} %mul.357, f32[512]{0:T(512)S(1)} %bitcast.84, f32[2048]{0:T(1024)S(1)} %mul.358, f32[512]{0:T(512)S(1)} %bitcast.85, f32[2048]{0:T(1024)S(1)} %mul.359, f32[512]{0:T(512)S(1)} %bitcast.83, f32[2048]{0:T(1024)S(1)} %mul.360), kind=kLoop, calls=%fused_computation.11.clone.1 | loop fusion | flops 9437184 | bytes 4233216 | tf_op jit(solution)/shard_map/while/body/eval_jaxpr/convert_element_type | solution.py:40
  193.5 16.2 %multiply_convert_fusion.3 = (bf16[512,2048]{1,0:T(8,128)(2,1)S(1)}, bf16[512,2048]{1,0:T(8,128)(2,1)S(1)}) fusion(f32[2048]{0:T(1024)S(1)} %mul.357, f32[512]{0:T(512)S(1)} %bitcast.84, f32[2048]{0:T(1024)S(1)} %mul.358, f32[512]{0:T(512)S(1)} %bitcast.85, f32[2048]{0:T(1024)S(1)} %mul.359, f32[512]{0:T(512)S(1)} %bitcast.83, f32[2048]{0:T(1024)S(1)} %mul.360), kind=kLoop, calls=%fused_computation.11.clone.1 | loop fusion | flops 9437184 | bytes 4233216 | tf_op jit(solution)/shard_map/while/body/eval_jaxpr/convert_element_type | solution.py:40
  211.6 16.2 %multiply_convert_fusion.3 = (bf16[512,2048]{1,0:T(8,128)(2,1)S(1)}, bf16[512,2048]{1,0:T(8,128)(2,1)S(1)}) fusion(f32[2048]{0:T(1024)S(1)} %mul.357, f32[512]{0:T(512)S(1)} %bitcast.84, f32[2048]{0:T(1024)S(1)} %mul.358, f32[512]{0:T(512)S(1)} %bitcast.85, f32[2048]{0:T(1024)S(1)} %mul.359, f32[512]{0:T(512)S(1)} %bitcast.83, f32[2048]{0:T(1024)S(1)} %mul.360), kind=kLoop, calls=%fused_computation.11.clone.1 | loop fusion | flops 9437184 | bytes 4233216 | tf_op jit(solution)/shard_map/while/body/eval_jaxpr/convert_element_type | solution.py:40
  229.7 16.2 %multiply_convert_fusion.3 = (bf16[512,2048]{1,0:T(8,128)(2,1)S(1)}, bf16[512,2048]{1,0:T(8,128)(2,1)S(1)}) fusion(f32[2048]{0:T(1024)S(1)} %mul.357, f32[512]{0:T(512)S(1)} %bitcast.84, f32[2048]{0:T(1024)S(1)} %mul.358, f32[512]{0:T(512)S(1)} %bitcast.85, f32[2048]{0:T(1024)S(1)} %mul.359, f32[512]{0:T(512)S(1)} %bitcast.83, f32[2048]{0:T(1024)S(1)} %mul.360), kind=kLoop, calls=%fused_computation.11.clone.1 | loop fusion | flops 9437184 | bytes 4233216 | tf_op jit(solution)/shard_map/while/body/eval_jaxpr/convert_element_type | solution.py:40
  247.8 16.2 %multiply_convert_fusion.3 = (bf16[512,2048]{1,0:T(8,128)(2,1)S(1)}, bf16[512,2048]{1,0:T(8,128)(2,1)S(1)}) fusion(f32[2048]{0:T(1024)S(1)} %mul.357, f32[512]{0:T(512)S(1)} %bitcast.84, f32[2048]{0:T(1024)S(1)} %mul.358, f32[512]{0:T(512)S(1)} %bitcast.85, f32[2048]{0:T(1024)S(1)} %mul.359, f32[512]{0:T(512)S(1)} %bitcast.83, f32[2048]{0:T(1024)S(1)} %mul.360), kind=kLoop, calls=%fused_computation.11.clone.1 | loop fusion | flops 9437184 | bytes 4233216 | tf_op jit(solution)/shard_map/while/body/eval_jaxpr/convert_element_type | solution.py:40
  265.9 16.2 %multiply_convert_fusion.3 = (bf16[512,2048]{1,0:T(8,128)(2,1)S(1)}, bf16[512,2048]{1,0:T(8,128)(2,1)S(1)}) fusion(f32[2048]{0:T(1024)S(1)} %mul.357, f32[512]{0:T(512)S(1)} %bitcast.84, f32[2048]{0:T(1024)S(1)} %mul.358, f32[512]{0:T(512)S(1)} %bitcast.85, f32[2048]{0:T(1024)S(1)} %mul.359, f32[512]{0:T(512)S(1)} %bitcast.83, f32[2048]{0:T(1024)S(1)} %mul.360), kind=kLoop, calls=%fused_computation.11.clone.1 | loop fusion | flops 9437184 | bytes 4233216 | tf_op jit(solution)/shard_map/while/body/eval_jaxpr/convert_element_type | solution.py:40
  284.0 16.2 %multiply_convert_fusion.3 = (bf16[512,2048]{1,0:T(8,128)(2,1)S(1)}, bf16[512,2048]{1,0:T(8,128)(2,1)S(1)}) fusion(f32[2048]{0:T(1024)S(1)} %mul.357, f32[512]{0:T(512)S(1)} %bitcast.84, f32[2048]{0:T(1024)S(1)} %mul.358, f32[512]{0:T(512)S(1)} %bitcast.85, f32[2048]{0:T(1024)S(1)} %mul.359, f32[512]{0:T(512)S(1)} %bitcast.83, f32[2048]{0:T(1024)S(1)} %mul.360), kind=kLoop, calls=%fused_computation.11.clone.1 | loop fusion | flops 9437184 | bytes 4233216 | tf_op jit(solution)/shard_map/while/body/eval_jaxpr/convert_element_type | solution.py:40
  302.1 16.2 %multiply_convert_fusion.3 = (bf16[512,2048]{1,0:T(8,128)(2,1)S(1)}, bf16[512,2048]{1,0:T(8,128)(2,1)S(1)}) fusion(f32[2048]{0:T(1024)S(1)} %mul.357, f32[512]{0:T(512)S(1)} %bitcast.84, f32[2048]{0:T(1024)S(1)} %mul.358, f32[512]{0:T(512)S(1)} %bitcast.85, f32[2048]{0:T(1024)S(1)} %mul.359, f32[512]{0:T(512)S(1)} %bitcast.83, f32[2048]{0:T(1024)S(1)} %mul.360), kind=kLoop, calls=%fused_computation.11.clone.1 | loop fusion | flops 9437184 | bytes 4233216 | tf_op jit(solution)/shard_map/while/body/eval_jaxpr/convert_element_type | solution.py:40
  320.2 16.2 %multiply_convert_fusion.3 = (bf16[512,2048]{1,0:T(8,128)(2,1)S(1)}, bf16[512,2048]{1,0:T(8,128)(2,1)S(1)}) fusion(f32[2048]{0:T(1024)S(1)} %mul.357, f32[512]{0:T(512)S(1)} %bitcast.84, f32[2048]{0:T(1024)S(1)} %mul.358, f32[512]{0:T(512)S(1)} %bitcast.85, f32[2048]{0:T(1024)S(1)} %mul.359, f32[512]{0:T(512)S(1)} %bitcast.83, f32[2048]{0:T(1024)S(1)} %mul.360), kind=kLoop, calls=%fused_computation.11.clone.1 | loop fusion | flops 9437184 | bytes 4233216 | tf_op jit(solution)/shard_map/while/body/eval_jaxpr/convert_element_type | solution.py:40
  338.3 16.2 %multiply_convert_fusion.3 = (bf16[512,2048]{1,0:T(8,128)(2,1)S(1)}, bf16[512,2048]{1,0:T(8,128)(2,1)S(1)}) fusion(f32[2048]{0:T(1024)S(1)} %mul.357, f32[512]{0:T(512)S(1)} %bitcast.84, f32[2048]{0:T(1024)S(1)} %mul.358, f32[512]{0:T(512)S(1)} %bitcast.85, f32[2048]{0:T(1024)S(1)} %mul.359, f32[512]{0:T(512)S(1)} %bitcast.83, f32[2048]{0:T(1024)S(1)} %mul.360), kind=kLoop, calls=%fused_computation.11.clone.1 | loop fusion | flops 9437184 | bytes 4233216 | tf_op jit(solution)/shard_map/while/body/eval_jaxpr/convert_element_type | solution.py:40
  356.4 16.2 %multiply_convert_fusion.3 = (bf16[512,2048]{1,0:T(8,128)(2,1)S(1)}, bf16[512,2048]{1,0:T(8,128)(2,1)S(1)}) fusion(f32[2048]{0:T(1024)S(1)} %mul.357, f32[512]{0:T(512)S(1)} %bitcast.84, f32[2048]{0:T(1024)S(1)} %mul.358, f32[512]{0:T(512)S(1)} %bitcast.85, f32[2048]{0:T(1024)S(1)} %mul.359, f32[512]{0:T(512)S(1)} %bitcast.83, f32[2048]{0:T(1024)S(1)} %mul.360), kind=kLoop, calls=%fused_computation.11.clone.1 | loop fusion | flops 9437184 | bytes 4233216 | tf_op jit(solution)/shard_map/while/body/eval_jaxpr/convert_element_type | solution.py:40
  374.5 16.2 %multiply_convert_fusion.3 = (bf16[512,2048]{1,0:T(8,128)(2,1)S(1)}, bf16[512,2048]{1,0:T(8,128)(2,1)S(1)}) fusion(f32[2048]{0:T(1024)S(1)} %mul.357, f32[512]{0:T(512)S(1)} %bitcast.84, f32[2048]{0:T(1024)S(1)} %mul.358, f32[512]{0:T(512)S(1)} %bitcast.85, f32[2048]{0:T(1024)S(1)} %mul.359, f32[512]{0:T(512)S(1)} %bitcast.83, f32[2048]{0:T(1024)S(1)} %mul.360), kind=kLoop, calls=%fused_computation.11.clone.1 | loop fusion | flops 9437184 | bytes 4233216 | tf_op jit(solution)/shard_map/while/body/eval_jaxpr/convert_element_type | solution.py:40
  392.6 16.2 %multiply_convert_fusion.3 = (bf16[512,2048]{1,0:T(8,128)(2,1)S(1)}, bf16[512,2048]{1,0:T(8,128)(2,1)S(1)}) fusion(f32[2048]{0:T(1024)S(1)} %mul.357, f32[512]{0:T(512)S(1)} %bitcast.84, f32[2048]{0:T(1024)S(1)} %mul.358, f32[512]{0:T(512)S(1)} %bitcast.85, f32[2048]{0:T(1024)S(1)} %mul.359, f32[512]{0:T(512)S(1)} %bitcast.83, f32[2048]{0:T(1024)S(1)} %mul.360), kind=kLoop, calls=%fused_computation.11.clone.1 | loop fusion | flops 9437184 | bytes 4233216 | tf_op jit(solution)/shard_map/while/body/eval_jaxpr/convert_element_type | solution.py:40
  410.7 16.2 %multiply_convert_fusion.3 = (bf16[512,2048]{1,0:T(8,128)(2,1)S(1)}, bf16[512,2048]{1,0:T(8,128)(2,1)S(1)}) fusion(f32[2048]{0:T(1024)S(1)} %mul.357, f32[512]{0:T(512)S(1)} %bitcast.84, f32[2048]{0:T(1024)S(1)} %mul.358, f32[512]{0:T(512)S(1)} %bitcast.85, f32[2048]{0:T(1024)S(1)} %mul.359, f32[512]{0:T(512)S(1)} %bitcast.83, f32[2048]{0:T(1024)S(1)} %mul.360), kind=kLoop, calls=%fused_computation.11.clone.1 | loop fusion | flops 9437184 | bytes 4233216 | tf_op jit(solution)/shard_map/while/body/eval_jaxpr/convert_element_type | solution.py:40
  429.6 48.6 %all_to_all.43 = bf16[32,256,128]{2,1,0:T(8,128)(2,1)S(1)} all-to-all(bf16[32,256,128]{2,1,0:T(8,128)(2,1)} %bitcast.77), channel_id=1, replica_groups=mesh['dir'=8,'box'=32] {'box'}, dimensions={0} | all-to-all | bytes 4194304 | tf_op jit(solution)/shard_map/all_to_all | solution.py:99
  478.2 11.1 %gather_fusion = bf16[2048,128]{1,0:T(8,128)(2,1)S(1)} fusion(bf16[32,256,128]{2,1,0:T(8,128)(2,1)S(1)} %all_to_all.43, s32[2048]{0:T(1024)S(1)} %bitcast.70), kind=kCustom, calls=%fused_computation | custom fusion | bytes 1064960 | tf_op jit(solution)/shard_map/gather | solution.py:100
  (223 shorter events, 66.3 us)
Async XLA Ops:
  4.9 7.5 %copy-start.5 = (s32[2048]{0:T(1024)S(1)}, s32[2048]{0:T(1024)}, u32[]{:S(2)}) copy-start(s32[2048]{0:T(1024)} %param.15) | copy-start | bytes 24580
  4.9 17.3 %copy-start.4 = (bf16[3,2048]{1,0:T(4,128)(2,1)S(1)}, bf16[3,2048]{1,0:T(4,128)(2,1)}, u32[]{:S(2)}) copy-start(bf16[3,2048]{1,0:T(4,128)(2,1)} %param.16) | copy-start | bytes 36868
  4.9 55.6 %all-to-all-start.1 = ((bf16[8,4,256,128]{3,0,1,2:T(8,128)(2,1)}), bf16[8,4,256,128]{3,0,1,2:T(8,128)(2,1)S(1)}, u32[]{:S(2)}, u32[]{:S(2)}) async-start(bf16[8,4,256,128]{3,0,1,2:T(8,128)(2,1)} %copy.68), calls=%async_computation.1 | async-start | bytes 4194304 | tf_op jit(solution)/shard_map/all_to_all | solution.py:57
  12.4 10.4 %copy-start.11 = (s32[2]{0:T(128)S(1)}, s32[2]{0:T(128)}, u32[]{:S(2)}) copy-start(s32[2]{0:T(128)} %constant.117) | copy-start | bytes 28
  12.4 10.5 %copy-start.10 = (s32[2]{0:T(128)S(1)}, s32[2]{0:T(128)}, u32[]{:S(2)}) copy-start(s32[2]{0:T(128)} %constant.120) | copy-start | bytes 28
  23.0 10.0 %copy-start.8 = (bf16[64,12]{0,1:T(8,128)(2,1)S(1)}, bf16[64,12]{0,1:T(8,128)(2,1)}, u32[]{:S(2)}) copy-start(bf16[64,12]{0,1:T(8,128)(2,1)} %param.13) | copy-start | bytes 4612
  23.1 10.1 %copy-start.6 = (s32[64,12]{0,1:T(8,128)S(1)}, s32[64,12]{0,1:T(8,128)}, u32[]{:S(2)}) copy-start(s32[64,12]{0,1:T(8,128)} %param.11) | copy-start | bytes 9220
  23.1 48.8 %copy-start.9 = (bf16[128,12]{0,1:T(8,128)(2,1)S(1)}, bf16[128,12]{0,1:T(8,128)(2,1)}, u32[]{:S(2)}) copy-start(bf16[128,12]{0,1:T(8,128)(2,1)} %param.14) | copy-start | bytes 9220
  23.1 48.8 %copy-start.7 = (s32[128,12]{0,1:T(8,128)S(1)}, s32[128,12]{0,1:T(8,128)}, u32[]{:S(2)}) copy-start(s32[128,12]{0,1:T(8,128)} %param.12) | copy-start | bytes 18436
  60.5 22.4 %all-to-all-start = ((bf16[32,256,4]{1,2,0:T(4,128)(2,1)}), bf16[32,256,4]{1,2,0:T(4,128)(2,1)S(1)}, u32[]{:S(2)}, u32[]{:S(2)}) async-start(bf16[32,256,4]{1,2,0:T(4,128)(2,1)} %copy.67), calls=%async_computation | async-start | bytes 131072 | tf_op jit(solution)/shard_map/all_to_all | solution.py:86
  82.9 52.7 %all-to-all-start.2 = ((bf16[64,4,32,128]{3,1,0,2:T(4,128)(2,1)}), bf16[64,4,32,128]{3,1,0,2:T(4,128)(2,1)S(1)}, u32[]{:S(2)}, u32[]{:S(2)}) async-start(bf16[64,4,32,128]{3,1,0,2:T(4,128)(2,1)} %copy.71), calls=%async_computation.2 | async-start | bytes 4194304 | tf_op jit(solution)/shard_map/all_to_all | solution.py:56
  137.1 1.6 copy-start
  428.3 1.3 copy-start.1
  478.2 11.1 %copy-start.3 = (bf16[2048,128]{1,0:T(8,128)(2,1)S(1)}, bf16[2048,128]{1,0:T(8,128)(2,1)}, u32[]{:S(2)}) copy-start(bf16[2048,128]{1,0:T(8,128)(2,1)} %param.17) | copy-start | bytes 1572868
  489.3 1.0 copy-start.2
where the time goes:
time: 491 us; the launch traced here: 490 us
  other arithmetic  273 us (56%)
  waiting for transfers between devices  82.8 us (17%)
  blocking collectives  48.6 us (10%)
  local copies, waits for them, and re-layouts  39.3 us (8%)
  starting transfers between devices  23 us (5%)
  matrix products  22 us (4%)
    convert_element_type x16, other arithmetic, field_rows(): cos_w = (quad[None, :] * jnp.cos(angle)).astype(jnp.bfloat16)  260 us
    all_to_all x1, blocking collectives, per_device(): lax.all_to_all(fields, 'box', split_axis=0, concat_axis=0, tiled=True)  48.6 us
    all_to_all x1, waiting for transfers between devices, per_device(): lax.all_to_all(lax.all_to_all(pattern, 'dir', split_axis=2, concat_axis=0...  47.8 us
    all_to_all x1, waiting for transfers between devices, per_device(): lax.all_to_all(pattern, 'dir', split_axis=2, concat_axis=0, tiled=True)  27.3 us
    dot_general x16, matrix products, field_rows(): return jnp.dot(phase, stacked, preferred_element_type=jnp.float32)  21.1 us
    unnamed x26, local copies, waits for them, and re-layouts  14.1 us
    all_to_all x1, starting transfers between devices, per_device(): lax.all_to_all(outgoing, 'box', split_axis=0, concat_axis=0, tiled=True)  11.3 us
    gather x1, local copies, waits for them, and re-layouts, per_device(): row_field = returned[dest, slot]  11.1 us
  transfers between devices with their start and end apart: 3, of which 3 were waited for; matrix products, arithmetic and copies ran while one was open for 5% of the time, Pallas kernels for 0%

commit v1 on v0

v1 whole, which is shorter than its diff:
```python
import functools
import math

import jax
import jax.numpy as jnp
import numpy as np
from jax import lax
from jax.experimental import pallas as pl
from jax.experimental.pallas import tpu as pltpu
from jax.sharding import PartitionSpec as P

NT = 64
NP = 128
NT_F = 32
NP_F = 64
C = 128
HALF = 64
N_DIR = 8
N_BOX = 32
N_XY = 16
ROW_DEV = 2048
SLOT = 64
HOT = 256
SLOTS = N_BOX * SLOT + HOT
P_DEV = NP // N_BOX
T_DEV = NT // N_DIR

box_phase = 50.265482

MESH = pl.DeviceIdType.MESH
BF = jnp.bfloat16
F32 = jnp.float32


def polynomials():
    z2 = 0.5 + 0.5 * np.cos(np.pi * (np.arange(400) + 0.5) / 400)
    z = np.sqrt(z2)
    s = np.polynomial.chebyshev.Chebyshev.fit(z2, np.sin(np.pi * z) / z, 7, domain=[0, 1])
    k = np.polynomial.chebyshev.Chebyshev.fit(z2, np.cos(np.pi * z), 8, domain=[0, 1])
    to = np.polynomial.polynomial.Polynomial
    return tuple(
        [float(v) for v in f.convert(kind=to, domain=[-1, 1], window=[-1, 1]).coef] for f in (s, k)
    )


SIN_POLY, COS_POLY = polynomials()


def turns(u):
    z = (u - jnp.round(u)) * 2.0
    w = z * z
    s = jnp.full_like(w, SIN_POLY[-1])
    for v in SIN_POLY[-2::-1]:
        s = s * w + v
    k = jnp.full_like(w, COS_POLY[-1])
    for v in COS_POLY[-2::-1]:
        k = k * w + v
    return k, s * z


def spread(taps, weights, count):
    grid = jnp.arange(count, dtype=jnp.int32)
    hit = taps[None, :, :] == grid[:, None, None]
    picked = jnp.where(hit, weights[None, :, :].astype(F32), F32(0.0))
    return jnp.sum(picked, axis=2).astype(BF)


def theta_signs():
    h = np.zeros((NT_F, NT_F), np.float32)
    for t in range(16):
        for c in range(2):
            h[c * 16 + t, t] = 1.0
            h[c * 16 + t, 31 - t] = (-1.0) ** c
    return h


def phi_signs():
    h = np.zeros((NP_F, NP_F), np.float32)
    for q in range(1, 16):
        for a in range(2):
            for b in range(2):
                r = q * 4 + a * 2 + b
                h[r, q] = 1.0
                h[r, 32 - q] = (-1.0) ** a
                h[r, 64 - q] = (-1.0) ** b
                h[r, 32 + q] = (-1.0) ** (a + b)
    for a in range(2):
        h[a * 2, 0] = 1.0
        h[a * 2, 32] = (-1.0) ** a
    h[1, 16], h[1, 48] = 1.0, -1.0
    h[3, 16], h[3, 48] = 1.0, 1.0
    return h


def prepare_kernel(ah, bh, rows, off, mt, mp, go, hotg, pos, geo, acc):
    box = rows[...]
    parent = box // 8
    octant = box - parent * 8
    dest = parent % N_BOX
    owner = lax.broadcasted_iota(jnp.int32, (N_BOX, ROW_DEV), 0)
    onehot = jnp.where(owner == dest, 1.0, 0.0).astype(F32)
    width = 256
    before = jnp.where(
        lax.broadcasted_iota(jnp.int32, (width, width), 0)
        < lax.broadcasted_iota(jnp.int32, (width, width), 1),
        1.0,
        0.0,
    ).astype(BF)
    carry = jnp.zeros((N_BOX, 1), F32)
    ranks = []
    for i in range(ROW_DEV // width):
        one = onehot[:, i * width : (i + 1) * width]
        pre = jnp.dot(one.astype(BF), before, preferred_element_type=F32) + carry
        ranks.append(jnp.sum(one * pre, axis=0, keepdims=True))
        carry = carry + jnp.sum(one, axis=1, keepdims=True)
    rank = jnp.concatenate(ranks, axis=1)
    is_hot = jnp.where(carry > float(SLOT), 1.0, 0.0)
    hot_row = jnp.sum(onehot * is_hot, axis=0, keepdims=True)
    number = lax.broadcasted_iota(jnp.int32, (N_BOX, 1), 0).astype(F32)
    hot = jnp.sum(number * is_hot, axis=0, keepdims=True)
    where_to = jnp.where(
        hot_row > 0.5, float(N_BOX * SLOT) + rank, dest.astype(F32) * float(SLOT) + rank
    )
    pos[...] = where_to
    col = lax.broadcasted_iota(jnp.int32, (NT, NT * N_XY), 1)
    row = lax.broadcasted_iota(jnp.int32, (NT, NT * N_XY), 0)
    wide = jnp.where(col // N_XY == row, 1.0, 0.0).astype(BF)
    v = jnp.dot(ah[...], wide, preferred_element_type=F32)
    lane_g = lax.broadcasted_iota(jnp.int32, v.shape, 1) % N_XY
    for g in range(N_XY):
        mt[g * NT_F : (g + 1) * NT_F, :] = jnp.where(lane_g == g, v, 0.0).astype(BF)
    half = lax.axis_index("box") // N_XY
    local = hot - (half * N_XY).astype(F32)
    mt[N_XY * NT_F :, :] = jnp.where(lane_g.astype(F32) == local, v, 0.0).astype(BF)
    col = lax.broadcasted_iota(jnp.int32, (NP, NP * 16), 1)
    row = lax.broadcasted_iota(jnp.int32, (NP, NP * 16), 0)
    wide = jnp.where(col // 16 == row, 1.0, 0.0).astype(BF)
    v = jnp.dot(bh[...], wide, preferred_element_type=F32)
    same = (
        lax.broadcasted_iota(jnp.int32, (16, NP * 16), 1) % 16
        == lax.broadcasted_iota(jnp.int32, (16, NP * 16), 0)
    )
    for r in range(NP_F):
        mp[r * 16 : (r + 1) * 16, :] = jnp.where(same, v[r : r + 1, :], 0.0).astype(BF)
    sub = lax.broadcasted_iota(jnp.int32, (16, ROW_DEV), 0)
    o = off[...].astype(F32)
    g = jnp.where(sub == 3, octant.astype(F32), 0.0)
    for i in range(3):
        g = jnp.where(sub == i, o[i : i + 1, :], g)
    geo[...] = g.astype(BF)
    acc[...] = jnp.zeros_like(acc)
    lane = lax.broadcasted_iota(jnp.int32, (128, 128), 1).astype(F32)

    def block(i, carry):
        at = pl.multiple_of(i * 256, 256)
        p = pos[:, pl.ds(at, 256)]
        oh = one_hot(p, lane)
        acc[...] += jnp.dot(geo[:, pl.ds(at, 256)], oh, preferred_element_type=F32)
        return carry

    lax.fori_loop(0, ROW_DEV // 256, block, 0)
    for m in range(N_BOX // 2):
        go[m] = acc[:, m * 128 : (m + 1) * 128].astype(BF)
    for m in range(2):
        hotg[m] = acc[:, N_BOX * SLOT + m * 128 : N_BOX * SLOT + (m + 1) * 128].astype(BF)


def one_hot(p, lane):
    parts = []
    for h in range(2):
        column = jnp.broadcast_to(p[:, h * 128 : (h + 1) * 128], (128, 128)).T
        parts.append(
            jnp.concatenate(
                [
                    jnp.where(column == lane + float(j * 128), 1.0, 0.0).astype(BF)
                    for j in range(SLOTS // 128)
                ],
                axis=1,
            )
        )
    return jnp.concatenate(parts, axis=0)


def prepare(ah, bh, rows, off):
    vm = pl.BlockSpec(memory_space=pltpu.VMEM)
    return pl.pallas_call(
        prepare_kernel,
        out_shape=(
            jax.ShapeDtypeStruct((N_XY * NT_F + NT_F, NT * N_XY), BF),
            jax.ShapeDtypeStruct((NP_F * 16, NP * 16), BF),
            jax.ShapeDtypeStruct((N_BOX // 2, 16, 128), BF),
            jax.ShapeDtypeStruct((2, 16, 128), BF),
            jax.ShapeDtypeStruct((1, ROW_DEV), F32),
        ),
        in_specs=[vm] * 4,
        out_specs=(vm,) * 5,
        scratch_shapes=[pltpu.VMEM((16, ROW_DEV), BF), pltpu.VMEM((16, SLOTS), F32)],
        compiler_params=pltpu.CompilerParams(vmem_limit_bytes=56 << 20),
        name="prepare",
    )(ah, bh, rows, off)


def exchange_kernel(
    pat, mt, go, ry, rh, rg, recv, ybuf, hbuf, twin, hsum,
    z_send, z_recv, z_self, g_send, g_recv, y_send, y_recv, t_send, t_recv, h_send, h_recv, self_sem,
):
    d = lax.axis_index("dir")
    b = lax.axis_index("box")
    zh = b // N_XY
    xy = b % N_XY
    e = zh * N_DIR + d

    barrier = pltpu.get_barrier_semaphore()

    def greet_z(k, carry):
        e2 = (e + k) % 16
        pl.semaphore_signal(
            barrier, inc=1, device_id=(e2 % N_DIR, e2 // N_DIR * N_XY + xy), device_id_type=MESH
        )
        return carry

    def greet_box(k, carry):
        pl.semaphore_signal(barrier, inc=1, device_id=(d, (b + k) % N_BOX), device_id_type=MESH)
        return carry

    lax.fori_loop(1, 16, greet_z, 0)
    lax.fori_loop(1, N_BOX, greet_box, 0)
    pl.semaphore_wait(barrier, 15 + N_BOX - 1)

    def z_copy(pi, k):
        e2 = (e + k) % 16
        d2, zh2 = e2 % N_DIR, e2 // N_DIR
        first = pl.multiple_of(d2 * N_BOX + zh2 * N_XY, N_XY)
        return pltpu.make_async_remote_copy(
            src_ref=pat.at[:, pi, pl.ds(first, N_XY), :],
            dst_ref=recv.at[pi, zh, d],
            send_sem=z_send.at[pi, k],
            recv_sem=z_recv.at[pi, k],
            device_id=(d2, zh2 * N_XY + xy),
            device_id_type=MESH,
        )

    def z_own(pi):
        first = pl.multiple_of(d * N_BOX + zh * N_XY, N_XY)
        return pltpu.make_async_copy(
            pat.at[:, pi, pl.ds(first, N_XY), :], recv.at[pi, zh, d], z_self.at[pi]
        )

    def g_copy(k):
        b2 = (b + k) % N_BOX
        return pltpu.make_async_remote_copy(
            src_ref=go.at[b2 // 2],
            dst_ref=rg.at[b],
            send_sem=g_send.at[k],
            recv_sem=g_recv.at[k],
            device_id=(d, b2),
            device_id_type=MESH,
        )

    def y_copy(pi, k):
        xy2 = (xy + k) % N_XY
        return pltpu.make_async_remote_copy(
            src_ref=ybuf.at[pi, xy2],
            dst_ref=ry.at[pi, xy],
            send_sem=y_send.at[pi, k],
            recv_sem=y_recv.at[pi, k],
            device_id=(d, zh * N_XY + xy2),
            device_id_type=MESH,
        )

    def h_copy(pi, k):
        xy2 = (xy + k) % N_XY
        return pltpu.make_async_remote_copy(
            src_ref=hsum.at[pi],
            dst_ref=rh.at[pi, xy],
            send_sem=h_send.at[pi, k],
            recv_sem=h_recv.at[pi, k],
            device_id=(d, zh * N_XY + xy2),
            device_id_type=MESH,
        )

    def t_copy(pi):
        return pltpu.make_async_remote_copy(
            src_ref=hbuf.at[pi],
            dst_ref=twin.at[pi],
            send_sem=t_send.at[pi],
            recv_sem=t_recv.at[pi],
            device_id=(d, (b + N_XY) % N_BOX),
            device_id_type=MESH,
        )

    def own_copies(pi):
        return (
            pltpu.make_async_copy(ybuf.at[pi, xy], ry.at[pi, xy], self_sem.at[0, pi]),
            pltpu.make_async_copy(hsum.at[pi], rh.at[pi, xy], self_sem.at[1, pi]),
        )

    own_geometry = pltpu.make_async_copy(go.at[b // 2], rg.at[b], self_sem.at[2, 0])

    def start(copy):
        return lambda k, carry: (copy(k).start(), carry)[1]

    def wait(copy):
        return lambda k, carry: (copy(k).wait(), carry)[1]

    def wait_recv(copy):
        return lambda k, carry: (copy(k).wait_recv(), carry)[1]

    def wait_send(copy):
        return lambda k, carry: (copy(k).wait_send(), carry)[1]

    lax.fori_loop(1, N_BOX, start(g_copy), 0)
    own_geometry.start()
    for pi in range(P_DEV):
        lax.fori_loop(1, 16, start(functools.partial(z_copy, pi)), 0)
        z_own(pi).start()

    def hot_step(pi):
        t_copy(pi).wait_recv()
        hsum[pi] = hbuf[pi] + twin[pi]
        lax.fori_loop(1, N_XY, start(functools.partial(h_copy, pi)), 0)
        own_copies(pi)[1].start()

    for pi in range(P_DEV):
        z_own(pi).wait()
        lax.fori_loop(1, 16, wait_recv(functools.partial(z_copy, pi)), 0)
        x = jnp.concatenate(
            [recv[pi, 0].reshape(NT * N_XY, C), recv[pi, 1].reshape(NT * N_XY, C)], axis=1
        )
        y = jnp.dot(mt[...], x, preferred_element_type=F32).astype(BF)
        for z in range(2):
            part = y[:, z * C : (z + 1) * C]
            ybuf[pi, :, z] = part[: N_XY * NT_F].reshape(N_XY, NT_F, C)
            hbuf[pi, z] = part[N_XY * NT_F :]
        t_copy(pi).start()
        lax.fori_loop(1, N_XY, start(functools.partial(y_copy, pi)), 0)
        own_copies(pi)[0].start()
        if pi:
            hot_step(pi - 1)
    hot_step(P_DEV - 1)
    own_geometry.wait()
    lax.fori_loop(1, N_BOX, wait(g_copy), 0)
    for pi in range(P_DEV):
        for copy in own_copies(pi):
            copy.wait()
        t_copy(pi).wait_send()
        lax.fori_loop(1, 16, wait_send(functools.partial(z_copy, pi)), 0)
        lax.fori_loop(1, N_XY, wait(functools.partial(y_copy, pi)), 0)
        lax.fori_loop(1, N_XY, wait(functools.partial(h_copy, pi)), 0)


def exchange(pattern, mt, go):
    vm = pl.BlockSpec(memory_space=pltpu.VMEM)
    anywhere = pl.BlockSpec(memory_space=pl.ANY)
    dma = pltpu.SemaphoreType.DMA
    theta = (P_DEV, N_XY, 2, NT_F, C)
    return pl.pallas_call(
        exchange_kernel,
        out_shape=(
            jax.ShapeDtypeStruct(theta, BF),
            jax.ShapeDtypeStruct(theta, BF),
            jax.ShapeDtypeStruct((N_BOX, 16, 128), BF),
        ),
        in_specs=[anywhere, vm, anywhere],
        out_specs=(anywhere,) * 3,
        scratch_shapes=[
            pltpu.VMEM((P_DEV, 2, N_DIR, T_DEV, N_XY, C), BF),
            pltpu.VMEM(theta, BF),
            pltpu.VMEM((P_DEV, 2, NT_F, C), BF),
            pltpu.VMEM((P_DEV, 2, NT_F, C), BF),
            pltpu.VMEM((P_DEV, 2, NT_F, C), BF),
            dma((P_DEV, 16)),
            dma((P_DEV, 16)),
            dma((P_DEV,)),
            dma((N_BOX,)),
            dma((N_BOX,)),
            dma((P_DEV, N_XY)),
            dma((P_DEV, N_XY)),
            dma((P_DEV,)),
            dma((P_DEV,)),
            dma((P_DEV, N_XY)),
            dma((P_DEV, N_XY)),
            dma((3, P_DEV)),
        ],
        compiler_params=pltpu.CompilerParams(
            collective_id=0, has_side_effects=True, vmem_limit_bytes=48 << 20
        ),
        name="exchange",
    )(pattern, mt, go)


def fields_kernel(ry, rh, mp, rg, hotg, sines, cosines, quad, out, xs, gt, gs, ex, ey):
    lane = lax.broadcasted_iota(jnp.int32, (16, C), 1)
    low = lane < HALF
    odd = lax.axis_index("box") % 2 == 1

    def side(m):
        t = rg[m].astype(F32)
        return jnp.where(odd, pltpu.roll(t, HALF, 1), t)

    for m in range(N_BOX // 2):
        second = pltpu.roll(side(2 * m + 1), HALF, 1)
        gs[:, m * 128 : (m + 1) * 128] = jnp.where(low, side(2 * m), second)
    for m in range(2):
        gs[:, N_BOX * SLOT + m * 128 : N_BOX * SLOT + (m + 1) * 128] = hotg[m].astype(F32)

    def directions(theta_part):
        for c in range(2):
            part = theta_part[:, :, :, c * 16 : (c + 1) * 16, :]
            xs[:, c * C : (c + 1) * C] = part.reshape(NP * 16, C)
        scale = quad[...]
        for piece in range(4):
            child = jnp.dot(
                mp[piece * 256 : (piece + 1) * 256, :], xs[...], preferred_element_type=F32
            )
            for r in range(4):
                q = piece * 4 + r
                parts = []
                for ab in range(4):
                    for c in range(2):
                        at = r * 64 + ab * 16
                        v = child[at : at + 16, c * C : (c + 1) * C] * scale
                        turn = (ab // 2 + ab % 2 + c) if (q or ab < 3) else c
                        if turn % 2:
                            v = pltpu.roll(v, HALF, 1)
                            v = jnp.where(low, -v, v) if turn == 1 else jnp.where(low, v, -v)
                        elif turn == 2:
                            v = -v
                        parts.append(v)
                gt[:, q * 128 : (q + 1) * 128] = jnp.concatenate(parts, axis=0).T.astype(BF)

    def rows(i, carry):
        at = pl.multiple_of(i * 256, 256)
        g = gs[:, pl.ds(at, 256)]
        octant = g[3:4]
        bz = jnp.where(octant >= 4.0, 1.0, 0.0)
        rest = octant - 4.0 * bz
        by = jnp.where(rest >= 2.0, 1.0, 0.0)
        bx = rest - 2.0 * by

        def turned(axis, bit):
            place = box_phase * ((2.0 * bit - 1.0) * 0.25 + g[axis : axis + 1] * 0.5)
            return place * (0.5 / math.pi)

        for table, u, factor in (
            (ex, turned(0, bx) * 0.5, sines),
            (ey, turned(1, by) * 0.5, cosines),
        ):
            k, s = turns(u * factor[...])
            table[0, 16:, :] = k
            table[1, 16:, :] = s
            table[0, :16, :] = k[16:]
            table[1, :16, :] = -s[16:]
        cc, sc = turns(turned(2, bz) * cosines[:16, :])
        total = jnp.zeros((C, 256), F32)
        for pair in range(8):
            parts = []
            for q in (2 * pair, 2 * pair + 1):
                lo, hi = 16 - q, 16 + q
                c1, s1 = ex[0, hi : hi + 16, :], ex[1, hi : hi + 16, :]
                c2, s2 = ex[0, lo : lo + 16, :], ex[1, lo : lo + 16, :]
                ca, sa = c1 * c2 - s1 * s2, s1 * c2 + c1 * s2
                if q == 0:
                    lo, hi = 0, 32
                c1, s1 = ey[0, hi : hi + 16, :], ey[1, hi : hi + 16, :]
                c2, s2 = ey[0, lo : lo + 16, :], ey[1, lo : lo + 16, :]
                cb, sb = c1 * c2 + s1 * s2, s2 * c1 - c2 * s1
                if q == 0:
                    four = (ca, sb, sa, cb)
                else:
                    four = (ca * cb, ca * sb, sa * cb, sa * sb)
                for v in four:
                    parts.append((v * cc).astype(BF))
                    parts.append((v * sc).astype(BF))
            w = jnp.concatenate(parts, axis=0)
            total = total + jnp.dot(
                gt[:, pair * 256 : (pair + 1) * 256], w, preferred_element_type=F32
            )
        out[pl.ds(at, 256), :] = total.T.astype(BF)
        return carry

    directions(ry)
    lax.fori_loop(0, N_BOX * SLOT // 256, rows, 0)
    directions(rh)
    lax.fori_loop(N_BOX * SLOT // 256, SLOTS // 256, rows, 0)


def fields(ry, rh, mp, rg, hotg):
    n = np.arange(NT_F) + 0.5
    wide = lambda v: jnp.asarray(np.repeat(v[:, None], 256, axis=1), F32)
    sines = wide(np.sin(np.pi * n / NT_F))
    cosines = wide(np.cos(np.pi * n / NT_F))
    quad = wide(np.sin(np.pi * n[:16] / NT_F) * math.sqrt(2.0 / (NT_F * NP_F)))[:, :C]
    vm = pl.BlockSpec(memory_space=pltpu.VMEM)
    return pl.pallas_call(
        fields_kernel,
        out_shape=jax.ShapeDtypeStruct((SLOTS, C), BF),
        in_specs=[vm] * 8,
        out_specs=vm,
        scratch_shapes=[
            pltpu.VMEM((NP * 16, 2 * C), BF),
            pltpu.VMEM((C, NT_F * NP_F), BF),
            pltpu.VMEM((16, SLOTS), F32),
            pltpu.VMEM((2, 48, 256), F32),
            pltpu.VMEM((2, 48, 256), F32),
        ],
        compiler_params=pltpu.CompilerParams(vmem_limit_bytes=56 << 20),
        name="fields",
    )(ry, rh, mp, rg, hotg, sines, cosines, quad)


def return_kernel(f, r, send, recv, own):
    d = lax.axis_index("dir")
    b = lax.axis_index("box")
    barrier = pltpu.get_barrier_semaphore()

    def greet(k, carry):
        pl.semaphore_signal(barrier, inc=1, device_id=(d, (b + k) % N_BOX), device_id_type=MESH)
        return carry

    lax.fori_loop(1, N_BOX, greet, 0)
    pl.semaphore_wait(barrier, N_BOX - 1)

    def copy(k):
        b2 = (b + k) % N_BOX
        return pltpu.make_async_remote_copy(
            src_ref=f.at[pl.ds(pl.multiple_of(b2 * SLOT, SLOT), SLOT), :],
            dst_ref=r.at[pl.ds(pl.multiple_of(b * SLOT, SLOT), SLOT), :],
            send_sem=send.at[k],
            recv_sem=recv.at[k],
            device_id=(d, b2),
            device_id_type=MESH,
        )

    at = pl.ds(pl.multiple_of(b * SLOT, SLOT), SLOT)
    mine = pltpu.make_async_copy(f.at[at, :], r.at[at, :], own)
    lax.fori_loop(1, N_BOX, lambda k, carry: (copy(k).start(), carry)[1], 0)
    mine.start()
    mine.wait()
    lax.fori_loop(1, N_BOX, lambda k, carry: (copy(k).wait(), carry)[1], 0)


def give_back(f):
    vm = pl.BlockSpec(memory_space=pltpu.VMEM)
    anywhere = pl.BlockSpec(memory_space=pl.ANY)
    return pl.pallas_call(
        return_kernel,
        out_shape=jax.ShapeDtypeStruct((N_BOX * SLOT, C), BF),
        in_specs=[vm],
        out_specs=anywhere,
        scratch_shapes=[
            pltpu.SemaphoreType.DMA((N_BOX,)),
            pltpu.SemaphoreType.DMA((N_BOX,)),
            pltpu.SemaphoreType.DMA,
        ],
        compiler_params=pltpu.CompilerParams(collective_id=1, has_side_effects=True),
        name="give_back",
    )(f)


def place_kernel(pos, r, f, out):
    lane = lax.broadcasted_iota(jnp.int32, (128, 128), 1).astype(F32)
    oh = one_hot(pos[...], lane)
    field = jnp.dot(oh[:, : N_BOX * SLOT], r[...], preferred_element_type=F32)
    field = field + jnp.dot(oh[:, N_BOX * SLOT :], f[...], preferred_element_type=F32)
    out[...] = field.astype(BF)


def place(pos, r, f):
    return pl.pallas_call(
        place_kernel,
        out_shape=jax.ShapeDtypeStruct((ROW_DEV, C), BF),
        grid=(ROW_DEV // 256,),
        in_specs=[
            pl.BlockSpec((1, 256), lambda i: (0, i)),
            pl.BlockSpec((N_BOX * SLOT, C), lambda i: (0, 0)),
            pl.BlockSpec((HOT, C), lambda i: (N_BOX * SLOT // HOT, 0)),
        ],
        out_specs=pl.BlockSpec((256, C), lambda i: (i, 0)),
        name="place",
    )(pos, r, f)


def per_device(pattern, tap_theta, tap_phi, weight_theta, weight_phi, row_box, row_offset, row_fwd):
    a_theta = spread(tap_theta, weight_theta, NT_F)
    a_phi = spread(tap_phi, weight_phi, NP_F)
    ah = jnp.dot(theta_signs().astype(BF), a_theta, preferred_element_type=F32).astype(BF)
    a_phi = a_phi.reshape(NP_F, 2, N_XY, P_DEV).transpose(0, 3, 2, 1).reshape(NP_F, NP)
    bh = jnp.dot(phi_signs().astype(BF), a_phi, preferred_element_type=F32).astype(BF)
    mt, mp, go, hotg, pos = prepare(ah, bh, row_box.reshape(1, ROW_DEV), row_offset)
    ry, rh, rg = exchange(pattern, mt, go)
    f = fields(ry, rh, mp, rg, hotg)
    r = give_back(f)
    row_field = place(pos, r, f)
    gradient = jnp.sum(row_fwd.astype(F32) * row_field.astype(F32), axis=1) * (0.5 / math.sqrt(C))
    return (row_field, gradient)


def solution(mesh):
    in_specs = (
        P("dir", "box", None, None),
        P(),
        P(),
        P(),
        P(),
        P(("dir", "box")),
        P(None, ("dir", "box")),
        P(("dir", "box"), None),
    )
    out_specs = (P(("dir", "box"), None), P(("dir", "box")))
    return jax.shard_map(
        per_device, mesh=mesh, in_specs=in_specs, out_specs=out_specs, check_vma=False
    )
```

time: 491 us -> 149 us (0.30)
  the two profiles are of different devices: /device:TPU:1 before, /device:TPU:32 now
where the time goes in v1:
time: 149 us; the launch traced here: 147 us
  Pallas kernels  132 us (89%)
  local copies, waits for them, and re-layouts  6.47 us (4%)
  other arithmetic  4.84 us (3%)
  matrix products  2.89 us (2%)
    pallas_call x1, Pallas kernels, exchange(): pl.pallas_call(exchange_kernel, out_shape=(jax.ShapeDtypeStruct(theta, BF...  83.1 us
    pallas_call x1, Pallas kernels, give_back(): pl.pallas_call(return_kernel, out_shape=jax.ShapeDtypeStruct((N_BOX * SLO...  19.3 us
    pallas_call x1, Pallas kernels, fields(): pl.pallas_call(fields_kernel, out_shape=jax.ShapeDtypeStruct((SLOTS, C),...  15.9 us
    pallas_call x1, Pallas kernels, prepare(): pl.pallas_call(prepare_kernel, out_shape=(jax.ShapeDtypeStruct((N_XY * NT...  7.08 us
    pallas_call x1, Pallas kernels, place(): pl.pallas_call(place_kernel, out_shape=jax.ShapeDtypeStruct((ROW_DEV, C),...  6.46 us
    unnamed x14, local copies, waits for them, and re-layouts  6.31 us

profile of v1, /device:TPU:32, one launch (start us, length us, event | category | flops | bytes accessed | tf_op | source)
XLA Modules:
  0.0 146.7 jit_solution(14337705504197328173)
XLA Ops:
  0.6 0.7 convert_element_type.34
  1.3 0.7 select_reduce_fusion.1
  2.1 1.4 fusion.1.ah
  3.5 0.7 convert_element_type.38
  4.2 0.7 select_reduce_fusion
  4.9 0.1 copy.24
  5.1 1.5 %fusion.bh = bf16[64,128]{1,0:T(8,128)(2,1)} fusion(bf16[64,128]{0,1:T(8,128)(2,1)S(1)} %bitcast.13, bf16[64,64]{1,0:T(8,128)(2,1)} %constant.15.clone), kind=kOutput, calls=%fused_computation.1 | convolution fusion | flops 1056768 | bytes 40960 | tf_op jit(solution)/shard_map/dot_general | solution.py:589
  6.5 7.1 %prepare.1 = (bf16[544,1024]{1,0:T(8,128)(2,1)}, bf16[1024,2048]{1,0:T(8,128)(2,1)}, bf16[16,16,128]{2,1,0:T(8,128)(2,1)}, bf16[2,16,128]{2,1,0:T(8,128)(2,1)}, f32[1,2048]{1,0:T(1,128)}) custom-call(bf16[32,64]{1,0:T(8,128)(2,1)} %fusion.1.ah, bf16[64,128]{1,0:T(8,128)(2,1)} %fusion.bh, s32[1,2048]{1,0:T(1,128)} %bitcast.15, bf16[3,2048]{1,0:T(4,128)(2,1)} %off.1), custom_call_target="tpu_custom_call" | custom-call | tf_op jit(solution)/shard_map/prepare/pallas_call | solution.py:186
  13.6 0.0 copy-start
  13.6 1.6 %copy-done = bf16[8,4,256,128]{3,2,1,0:T(8,128)(2,1)S(1)} copy-done((bf16[8,4,256,128]{3,2,1,0:T(8,128)(2,1)S(1)}, bf16[8,4,256,128]{3,2,1,0:T(8,128)(2,1)}, u32[]{:S(2)}) %copy-start) | copy-done | bytes 2097176
  15.2 0.0 copy-start.1
  15.2 1.2 copy-done.1
  16.5 0.8 copy-done.5
  17.3 83.1 %exchange.1 = (bf16[4,16,2,32,128]{4,3,2,1,0:T(8,128)(2,1)S(1)}, bf16[4,16,2,32,128]{4,3,2,1,0:T(8,128)(2,1)S(1)}, bf16[32,16,128]{2,1,0:T(8,128)(2,1)S(1)}) custom-call(bf16[8,4,256,128]{3,2,1,0:T(8,128)(2,1)S(1)} %copy-done, bf16[544,1024]{1,0:T(8,128)(2,1)S(1)} %copy-done.1, bf16[16,16,128]{2,1,0:T(8,128)(2,1)S(1)} %copy-done.5), custom_call_target="tpu_custom_call" | custom-call | tf_op jit(solution)/shard_map/exchange/pallas_call | solution.py:357
  100.4 0.0 copy-start.2
  100.4 1.0 copy-done.2
  101.4 1.0 copy-done.3
  102.4 0.7 copy-done.4
  103.0 15.9 %fields.1.f = bf16[2304,128]{1,0:T(8,128)(2,1)} custom-call(bf16[4,16,2,32,128]{4,3,2,1,0:T(8,128)(2,1)} %copy-done.2, bf16[4,16,2,32,128]{4,3,2,1,0:T(8,128)(2,1)} %copy-done.3, bf16[1024,2048]{1,0:T(8,128)(2,1)} %get-tuple-element.15.mp, bf16[32,16,128]{2,1,0:T(8,128)(2,1)} %copy-done.4, bf16[2,16,128]{2,1,0:T(8,128)(2,1)} %get-tuple-element.17.hotg, ...), custom_call_target="tpu_custom_call" | custom-call | tf_op jit(solution)/shard_map/fields/pallas_call | solution.py:495
  118.9 19.3 %give_back.1.r = bf16[2048,128]{1,0:T(8,128)(2,1)} custom-call(bf16[2304,128]{1,0:T(8,128)(2,1)} %fields.1.f), custom_call_target="tpu_custom_call" | custom-call | tf_op jit(solution)/shard_map/give_back/pallas_call | solution.py:546
  138.2 6.5 %place.1 = bf16[2048,128]{1,0:T(8,128)(2,1)} custom-call(f32[1,2048]{1,0:T(1,128)} %get-tuple-element.10.pos, bf16[2048,128]{1,0:T(8,128)(2,1)} %give_back.1.r, bf16[2304,128]{1,0:T(8,128)(2,1)} %fields.1.f), custom_call_target="tpu_custom_call" | custom-call | tf_op jit(solution)/shard_map/place/pallas_call | solution.py:570
  144.7 0.0 copy-done.6
  144.7 1.4 multiply_reduce_fusion
  146.0 0.6 broadcast_multiply_fusion
  (5 shorter events, 0.0 us)
Async XLA Ops:
  13.6 1.6 %copy-start = (bf16[8,4,256,128]{3,2,1,0:T(8,128)(2,1)S(1)}, bf16[8,4,256,128]{3,2,1,0:T(8,128)(2,1)}, u32[]{:S(2)}) copy-start(bf16[8,4,256,128]{3,2,1,0:T(8,128)(2,1)} %pat.1) | copy-start | bytes 6291460
  15.2 1.2 copy-start.1
  16.5 0.8 copy-start.5
  100.4 1.0 copy-start.2
  101.4 1.0 copy-start.3
  102.4 0.7 copy-start.4
  118.9 25.7 %copy-start.6 = (bf16[2048,128]{1,0:T(8,128)(2,1)S(1)}, bf16[2048,128]{1,0:T(8,128)(2,1)}, u32[]{:S(2)}) copy-start(bf16[2048,128]{1,0:T(8,128)(2,1)} %param.20) | copy-start | bytes 1572868

commit v2 on v0

v2 whole, which is shorter than its diff:
```python
import functools
import math

import jax
import jax.numpy as jnp
import numpy as np
from jax import lax
from jax.experimental import pallas as pl
from jax.experimental.pallas import tpu as pltpu
from jax.sharding import PartitionSpec as P

NT = 64
NP = 128
NT_F = 32
NP_F = 64
C = 128
HALF = 64
N_DIR = 8
N_BOX = 32
N_XY = 16
ROW_DEV = 2048
SLOT = 64
HOT = 256
SLOTS = N_BOX * SLOT + HOT
P_DEV = NP // N_BOX
T_DEV = NT // N_DIR

box_phase = 50.265482

MESH = pl.DeviceIdType.MESH
BF = jnp.bfloat16
F32 = jnp.float32


def polynomials():
    z2 = 0.5 + 0.5 * np.cos(np.pi * (np.arange(400) + 0.5) / 400)
    z = np.sqrt(z2)
    s = np.polynomial.chebyshev.Chebyshev.fit(z2, np.sin(np.pi * z) / z, 7, domain=[0, 1])
    k = np.polynomial.chebyshev.Chebyshev.fit(z2, np.cos(np.pi * z), 8, domain=[0, 1])
    to = np.polynomial.polynomial.Polynomial
    return tuple(
        [float(v) for v in f.convert(kind=to, domain=[-1, 1], window=[-1, 1]).coef] for f in (s, k)
    )


SIN_POLY, COS_POLY = polynomials()


def turns(u):
    z = (u - jnp.round(u)) * 2.0
    w = z * z
    s = jnp.full_like(w, SIN_POLY[-1])
    for v in SIN_POLY[-2::-1]:
        s = s * w + v
    k = jnp.full_like(w, COS_POLY[-1])
    for v in COS_POLY[-2::-1]:
        k = k * w + v
    return k, s * z


def theta_signs():
    h = np.zeros((NT_F, NT_F), np.float32)
    for t in range(16):
        for c in range(2):
            h[c * 16 + t, t] = 1.0
            h[c * 16 + t, 31 - t] = (-1.0) ** c
    return h


def phi_signs():
    h = np.zeros((NP_F, NP_F), np.float32)
    for q in range(1, 16):
        for a in range(2):
            for b in range(2):
                r = q * 4 + a * 2 + b
                h[r, q] = 1.0
                h[r, 32 - q] = (-1.0) ** a
                h[r, 64 - q] = (-1.0) ** b
                h[r, 32 + q] = (-1.0) ** (a + b)
    for a in range(2):
        h[a * 2, 0] = 1.0
        h[a * 2, 32] = (-1.0) ** a
    h[1, 16], h[1, 48] = 1.0, -1.0
    h[3, 16], h[3, 48] = 1.0, 1.0
    return h


def one_hot(p, lane):
    parts = []
    for h in range(2):
        column = jnp.broadcast_to(p[:, h * 128 : (h + 1) * 128], (128, 128)).T
        parts.append(
            jnp.concatenate(
                [
                    jnp.where(column == lane + float(j * 128), 1.0, 0.0).astype(BF)
                    for j in range(SLOTS // 128)
                ],
                axis=1,
            )
        )
    return jnp.concatenate(parts, axis=0)


def spread(taps, weights):
    lane = lax.broadcasted_iota(jnp.int32, (taps.shape[0], 128), 1)
    total = jnp.zeros(lane.shape, F32)
    for j in range(taps.shape[1]):
        total = total + jnp.where(
            lane == taps[:, j : j + 1], weights[:, j : j + 1].astype(F32), 0.0
        )
    return total


def step_kernel(
    pat, tap_t, tap_p, wt_t, wt_p, sign_t, sign_p, box_of_row, off, fwd, sines, cosines, quad,
    field, grad,
    recv, ybuf, hbuf, twin, hsum, ry, rh, go, hotg, rg, mt, mp, geo, gacc, oh, gs, ex, ey, w,
    acc_own, acc_hot, gt, f, r, fwd_v,
    z_send, z_recv, z_self, g_send, g_recv, y_send, y_recv, t_send, t_recv, h_send, h_recv, self_sem,
    r_send, r_recv, r_self, fwd_sem,
):
    d = lax.axis_index("dir")
    b = lax.axis_index("box")
    zh = b // N_XY
    xy = b % N_XY
    e = zh * N_DIR + d

    barrier = pltpu.get_barrier_semaphore()

    def greet_z(k, carry):
        e2 = (e + k) % 16
        pl.semaphore_signal(
            barrier, inc=1, device_id=(e2 % N_DIR, e2 // N_DIR * N_XY + xy), device_id_type=MESH
        )
        return carry

    def greet_box(k, carry):
        pl.semaphore_signal(barrier, inc=1, device_id=(d, (b + k) % N_BOX), device_id_type=MESH)
        return carry

    lax.fori_loop(1, 16, greet_z, 0)
    lax.fori_loop(1, N_BOX, greet_box, 0)
    pl.semaphore_wait(barrier, 15 + N_BOX - 1)


    def z_copy(pi, k):
        e2 = (e + k) % 16
        d2, zh2 = e2 % N_DIR, e2 // N_DIR
        first = pl.multiple_of(d2 * N_BOX + zh2 * N_XY, N_XY)
        return pltpu.make_async_remote_copy(
            src_ref=pat.at[:, pi, pl.ds(first, N_XY), :],
            dst_ref=recv.at[pi, zh, d],
            send_sem=z_send.at[pi, k],
            recv_sem=z_recv.at[pi, k],
            device_id=(d2, zh2 * N_XY + xy),
            device_id_type=MESH,
        )

    def z_own(pi):
        first = pl.multiple_of(d * N_BOX + zh * N_XY, N_XY)
        return pltpu.make_async_copy(
            pat.at[:, pi, pl.ds(first, N_XY), :], recv.at[pi, zh, d], z_self.at[pi]
        )

    def g_copy(k):
        b2 = (b + k) % N_BOX
        return pltpu.make_async_remote_copy(
            src_ref=go.at[b2 // 2],
            dst_ref=rg.at[b],
            send_sem=g_send.at[k],
            recv_sem=g_recv.at[k],
            device_id=(d, b2),
            device_id_type=MESH,
        )

    def y_copy(pi, k):
        xy2 = (xy + k) % N_XY
        return pltpu.make_async_remote_copy(
            src_ref=ybuf.at[pi, xy2],
            dst_ref=ry.at[pi, xy],
            send_sem=y_send.at[pi, k],
            recv_sem=y_recv.at[pi, k],
            device_id=(d, zh * N_XY + xy2),
            device_id_type=MESH,
        )

    def h_copy(pi, k):
        xy2 = (xy + k) % N_XY
        return pltpu.make_async_remote_copy(
            src_ref=hsum.at[pi],
            dst_ref=rh.at[pi, xy],
            send_sem=h_send.at[pi, k],
            recv_sem=h_recv.at[pi, k],
            device_id=(d, zh * N_XY + xy2),
            device_id_type=MESH,
        )

    def t_copy(pi):
        return pltpu.make_async_remote_copy(
            src_ref=hbuf.at[pi],
            dst_ref=twin.at[pi],
            send_sem=t_send.at[pi],
            recv_sem=t_recv.at[pi],
            device_id=(d, (b + N_XY) % N_BOX),
            device_id_type=MESH,
        )

    def y_own(pi):
        return pltpu.make_async_copy(ybuf.at[pi, xy], ry.at[pi, xy], self_sem.at[0, pi])

    def h_own(pi):
        return pltpu.make_async_copy(hsum.at[pi], rh.at[pi, xy], self_sem.at[1, pi])

    def g_own():
        return pltpu.make_async_copy(go.at[b // 2], rg.at[b], self_sem.at[2, 0])

    def r_copy(b2):
        return pltpu.make_async_remote_copy(
            src_ref=f.at[pl.ds(pl.multiple_of(b2 * SLOT, SLOT), SLOT), :],
            dst_ref=r.at[pl.ds(pl.multiple_of(b * SLOT, SLOT), SLOT), :],
            send_sem=r_send.at[b2],
            recv_sem=r_recv.at[b],
            device_id=(d, b2),
            device_id_type=MESH,
        )

    def r_arrival(b2):
        return pltpu.make_async_remote_copy(
            src_ref=f.at[pl.ds(pl.multiple_of(b2 * SLOT, SLOT), SLOT), :],
            dst_ref=r.at[pl.ds(pl.multiple_of(b2 * SLOT, SLOT), SLOT), :],
            send_sem=r_send.at[b2],
            recv_sem=r_recv.at[b2],
            device_id=(d, b2),
            device_id_type=MESH,
        )

    def r_own():
        at = pl.ds(pl.multiple_of(b * SLOT, SLOT), SLOT)
        return pltpu.make_async_copy(f.at[at, :], r.at[at, :], r_self)

    def load_fwd():
        return pltpu.make_async_copy(fwd, fwd_v, fwd_sem)

    def each(n, copy, what):
        def one(k, carry):
            getattr(copy(k), what)()
            return carry

        lax.fori_loop(1, n, one, 0)

    for pi in range(P_DEV):
        each(16, functools.partial(z_copy, pi), "start")
        z_own(pi).start()
    load_fwd().start()


    box = box_of_row[...]
    parent = box // 8
    octant = box - parent * 8
    dest = parent % N_BOX
    owner = lax.broadcasted_iota(jnp.int32, (N_BOX, ROW_DEV), 0)
    onehot = jnp.where(owner == dest, 1.0, 0.0).astype(F32)
    width = 256
    before = jnp.where(
        lax.broadcasted_iota(jnp.int32, (width, width), 0)
        < lax.broadcasted_iota(jnp.int32, (width, width), 1),
        1.0,
        0.0,
    ).astype(BF)
    carry = jnp.zeros((N_BOX, 1), F32)
    ranks = []
    for i in range(ROW_DEV // width):
        one = onehot[:, i * width : (i + 1) * width]
        pre = jnp.dot(one.astype(BF), before, preferred_element_type=F32) + carry
        ranks.append(jnp.sum(one * pre, axis=0, keepdims=True))
        carry = carry + jnp.sum(one, axis=1, keepdims=True)
    rank = jnp.concatenate(ranks, axis=1)
    is_hot = jnp.where(carry > float(SLOT), 1.0, 0.0)
    hot_row = jnp.sum(onehot * is_hot, axis=0, keepdims=True)
    number = lax.broadcasted_iota(jnp.int32, (N_BOX, 1), 0).astype(F32)
    hot = jnp.sum(number * is_hot, axis=0, keepdims=True)
    pos = jnp.where(
        hot_row > 0.5, float(N_BOX * SLOT) + rank, dest.astype(F32) * float(SLOT) + rank
    )
    sub = lax.broadcasted_iota(jnp.int32, (16, ROW_DEV), 0)
    o = off[...].astype(F32)
    g = jnp.where(sub == 3, octant.astype(F32), 0.0)
    for i in range(3):
        g = jnp.where(sub == i, o[i : i + 1, :], g)
    g = g.astype(BF)
    for i in range(ROW_DEV // width):
        geo[i, :16] = g[:, i * width : (i + 1) * width].astype(F32)
        geo[i, 16:] = jnp.broadcast_to(pos[:, i * width : (i + 1) * width], (8, width))
    gacc[...] = jnp.zeros_like(gacc)
    lane128 = lax.broadcasted_iota(jnp.int32, (128, 128), 1).astype(F32)

    def sort_block(i, carry):
        hits = one_hot(geo[i, 16:17], lane128)
        oh[i] = hits
        gacc[...] += jnp.dot(geo[i, :16].astype(BF), hits, preferred_element_type=F32)
        return carry

    lax.fori_loop(0, ROW_DEV // width, sort_block, 0)
    for m in range(N_BOX // 2):
        go[m] = gacc[:, m * 128 : (m + 1) * 128].astype(BF)
    for m in range(2):
        hotg[m] = gacc[:, N_BOX * SLOT + m * 128 : N_BOX * SLOT + (m + 1) * 128]
    each(N_BOX, g_copy, "start")
    g_own().start()


    a_theta = spread(tap_t[...], wt_t[...]).T[:NT_F].astype(BF)
    ah = jnp.dot(sign_t[...], a_theta, preferred_element_type=F32).astype(BF)
    col = lax.broadcasted_iota(jnp.int32, (NT, NT * N_XY), 1)
    row = lax.broadcasted_iota(jnp.int32, (NT, NT * N_XY), 0)
    wide = jnp.where(col // N_XY == row, 1.0, 0.0).astype(BF)
    v = jnp.dot(ah, wide, preferred_element_type=F32)
    lane_g = lax.broadcasted_iota(jnp.int32, v.shape, 1) % N_XY
    for i in range(N_XY):
        mt[i * NT_F : (i + 1) * NT_F, :] = jnp.where(lane_g == i, v, 0.0).astype(BF)
    local = hot - (zh * N_XY).astype(F32)
    mt[N_XY * NT_F :, :] = jnp.where(lane_g.astype(F32) == local, v, 0.0).astype(BF)

    a_phi = spread(tap_p[...], wt_p[...]).T[:NP_F].astype(BF)
    bh = jnp.dot(sign_p[...], a_phi, preferred_element_type=F32).astype(BF)
    col = lax.broadcasted_iota(jnp.int32, (NP, NP * 16), 1) // 16
    row = lax.broadcasted_iota(jnp.int32, (NP, NP * 16), 0)
    sample = col % 2 * (NP // 2) + col // 2 % N_XY * P_DEV + col // N_BOX
    wide = jnp.where(sample == row, 1.0, 0.0).astype(BF)
    v = jnp.dot(bh, wide, preferred_element_type=F32)
    same = (
        lax.broadcasted_iota(jnp.int32, (16, NP * 16), 1) % 16
        == lax.broadcasted_iota(jnp.int32, (16, NP * 16), 0)
    )
    for i in range(NP_F):
        mp[i * 16 : (i + 1) * 16, :] = jnp.where(same, v[i : i + 1, :], 0.0).astype(BF)


    lane = lax.broadcasted_iota(jnp.int32, (16, C), 1)
    low = lane < HALF

    def gather_geometry():
        g_own().wait()
        each(N_BOX, g_copy, "wait_recv")
        odd = b % 2 == 1

        def side(m):
            t = rg[m].astype(F32)
            return jnp.where(odd, pltpu.roll(t, HALF, 1), t)

        for m in range(N_BOX // 2):
            second = pltpu.roll(side(2 * m + 1), HALF, 1)
            gs[m // 2, :, m % 2 * 128 : (m % 2 + 1) * 128] = jnp.where(low, side(2 * m), second)
        for m in range(2):
            gs[N_BOX // 4, :, m * 128 : (m + 1) * 128] = hotg[m]

    def phases(i, carry):
        g = gs[i]
        octant = g[3:4]
        bz = jnp.where(octant >= 4.0, 1.0, 0.0)
        rest = octant - 4.0 * bz
        by = jnp.where(rest >= 2.0, 1.0, 0.0)
        bx = rest - 2.0 * by

        def turned(axis, bit):
            place = box_phase * ((2.0 * bit - 1.0) * 0.25 + g[axis : axis + 1] * 0.5)
            return place * (0.5 / math.pi)

        for table, u, factor in (
            (ex, turned(0, bx) * 0.5, sines),
            (ey, turned(1, by) * 0.5, cosines),
        ):
            k, s = turns(u * factor[...])
            table[0, 16:, :] = k
            table[1, 16:, :] = s
            table[0, :16, :] = k[16:]
            table[1, :16, :] = -s[16:]
        cc, sc = turns(turned(2, bz) * cosines[:16, :])
        for q in range(16):
            lo, hi = 16 - q, 16 + q
            c1, s1 = ex[0, hi : hi + 16, :], ex[1, hi : hi + 16, :]
            c2, s2 = ex[0, lo : lo + 16, :], ex[1, lo : lo + 16, :]
            ca, sa = c1 * c2 - s1 * s2, s1 * c2 + c1 * s2
            if q == 0:
                lo, hi = 0, 32
            c1, s1 = ey[0, hi : hi + 16, :], ey[1, hi : hi + 16, :]
            c2, s2 = ey[0, lo : lo + 16, :], ey[1, lo : lo + 16, :]
            cb, sb = c1 * c2 + s1 * s2, s2 * c1 - c2 * s1
            if q == 0:
                four = (ca, sb, sa, cb)
            else:
                four = (ca * cb, ca * sb, sa * cb, sa * sb)
            for j, v in enumerate(four):
                at = q * 128 + j * 32
                w[i, at : at + 16, :] = (v * cc).astype(BF)
                w[i, at + 16 : at + 32, :] = (v * sc).astype(BF)
        return carry


    def theta_step(pi):
        z_own(pi).wait()
        each(16, functools.partial(z_copy, pi), "wait_recv")
        x = jnp.concatenate(
            [recv[pi, 0].reshape(NT * N_XY, C), recv[pi, 1].reshape(NT * N_XY, C)], axis=1
        )
        y = jnp.dot(mt[...], x, preferred_element_type=F32).astype(BF)
        for z in range(2):
            part = y[:, z * C : (z + 1) * C]
            ybuf[pi, :, z] = part[: N_XY * NT_F].reshape(N_XY, NT_F, C)
            hbuf[pi, z] = part[N_XY * NT_F :]
        each(N_XY, functools.partial(y_copy, pi), "start")
        t_copy(pi).start()
        y_own(pi).start()

    def hot_step(pi):
        t_copy(pi).wait_recv()
        hsum[pi] = hbuf[pi] + twin[pi]
        each(N_XY, functools.partial(h_copy, pi), "start")
        h_own(pi).start()

    def phi_step(pi, part, own, copy, acc):
        own(pi).wait()
        each(N_XY, functools.partial(copy, pi), "wait_recv")
        x = jnp.concatenate(
            [part[pi, :, :, c * 16 : (c + 1) * 16, :].reshape(512, C) for c in range(2)], axis=1
        )
        y = jnp.dot(mp[:, pi * 512 : (pi + 1) * 512], x, preferred_element_type=F32)
        if pi:
            acc[...] += y
        else:
            acc[...] = y

    def directions(acc):
        scale = quad[...]
        for q in range(16):
            parts = []
            for ab in range(4):
                for c in range(2):
                    at = q * 64 + ab * 16
                    v = acc[at : at + 16, c * C : (c + 1) * C] * scale
                    turn = (ab // 2 + ab % 2 + c) if (q or ab < 3) else c
                    if turn % 2:
                        v = pltpu.roll(v, HALF, 1)
                        v = jnp.where(low, -v, v) if turn == 1 else jnp.where(low, v, -v)
                    elif turn == 2:
                        v = -v
                    parts.append(v)
            gt[:, q * 128 : (q + 1) * 128] = jnp.concatenate(parts, axis=0).T.astype(BF)

    def field_block(i):
        return jnp.dot(gt[...], w[i], preferred_element_type=F32).T.astype(BF)

    def send_block(i, carry):
        at = (b // 4 + i) % (N_BOX // 4)
        f[pl.ds(pl.multiple_of(at * 256, 256), 256), :] = field_block(at)
        for j in range(4):
            b2 = at * 4 + j

            @pl.when(b2 != b)
            def _():
                r_copy(b2).start()

            @pl.when(b2 == b)
            def _():
                r_own().start()

        return carry

    own_args = (ry, y_own, y_copy, acc_own)
    hot_args = (rh, h_own, h_copy, acc_hot)
    theta_step(0)
    gather_geometry()
    lax.fori_loop(0, 3, phases, 0)
    hot_step(0)
    theta_step(1)
    phi_step(0, *own_args)
    lax.fori_loop(3, 6, phases, 0)
    hot_step(1)
    theta_step(2)
    phi_step(1, *own_args)
    phi_step(0, *hot_args)
    lax.fori_loop(6, 9, phases, 0)
    hot_step(2)
    theta_step(3)
    phi_step(2, *own_args)
    phi_step(1, *hot_args)
    hot_step(3)
    phi_step(3, *own_args)
    directions(acc_own)
    lax.fori_loop(0, N_BOX // 4, send_block, 0)
    phi_step(2, *hot_args)
    phi_step(3, *hot_args)
    directions(acc_hot)
    f[N_BOX * SLOT :, :] = field_block(N_BOX // 4)
    load_fwd().wait()
    r_own().wait()

    def arrived(k, carry):
        r_arrival((b + k) % N_BOX).wait_recv()
        return carry

    lax.fori_loop(1, N_BOX, arrived, 0)

    def place(i, carry):
        hits = oh[i]
        v = jnp.dot(hits[:, : N_BOX * SLOT], r[...], preferred_element_type=F32)
        v = v + jnp.dot(hits[:, N_BOX * SLOT :], f[N_BOX * SLOT :, :], preferred_element_type=F32)
        v = v.astype(BF)
        at = pl.multiple_of(i * 256, 256)
        field[pl.ds(at, 256), :] = v
        product = fwd_v[pl.ds(at, 256), :].astype(F32) * v.astype(F32)
        grad[:, pl.ds(at, 256)] = jnp.sum(product.T, axis=0, keepdims=True) * (0.5 / math.sqrt(C))
        return carry

    lax.fori_loop(0, ROW_DEV // 256, place, 0)
    each(N_BOX, g_copy, "wait_send")
    for pi in range(P_DEV):
        t_copy(pi).wait_send()
        each(16, functools.partial(z_copy, pi), "wait_send")
        each(N_XY, functools.partial(y_copy, pi), "wait_send")
        each(N_XY, functools.partial(h_copy, pi), "wait_send")

    def sent(k, carry):
        r_copy((b + k) % N_BOX).wait_send()
        return carry

    lax.fori_loop(1, N_BOX, sent, 0)


def step(pattern, tap_theta, tap_phi, weight_theta, weight_phi, row_box, row_offset, row_fwd):
    n = np.arange(NT_F) + 0.5
    wide = lambda v: jnp.asarray(np.repeat(v[:, None], 256, axis=1), F32)
    sines = wide(np.sin(np.pi * n / NT_F))
    cosines = wide(np.cos(np.pi * n / NT_F))
    quad = wide(np.sin(np.pi * n[:16] / NT_F) * math.sqrt(2.0 / (NT_F * NP_F)))[:, :C]
    vm = pl.BlockSpec(memory_space=pltpu.VMEM)
    anywhere = pl.BlockSpec(memory_space=pl.ANY)
    dma = pltpu.SemaphoreType.DMA
    theta = (P_DEV, N_XY, 2, NT_F, C)
    hot = (P_DEV, 2, NT_F, C)
    blocks = SLOTS // 256
    return pl.pallas_call(
        step_kernel,
        out_shape=(
            jax.ShapeDtypeStruct((ROW_DEV, C), BF),
            jax.ShapeDtypeStruct((1, ROW_DEV), F32),
        ),
        in_specs=[anywhere] + [vm] * 8 + [anywhere] + [vm] * 3,
        out_specs=(vm, vm),
        scratch_shapes=[
            pltpu.VMEM((P_DEV, 2, N_DIR, T_DEV, N_XY, C), BF),
            pltpu.VMEM(theta, BF),
            pltpu.VMEM(hot, BF),
            pltpu.VMEM(hot, BF),
            pltpu.VMEM(hot, BF),
            pltpu.VMEM(theta, BF),
            pltpu.VMEM(theta, BF),
            pltpu.VMEM((N_BOX // 2, 16, 128), BF),
            pltpu.VMEM((2, 16, 128), F32),
            pltpu.VMEM((N_BOX, 16, 128), BF),
            pltpu.VMEM((N_XY * NT_F + NT_F, NT * N_XY), BF),
            pltpu.VMEM((NP_F * 16, NP * 16), BF),
            pltpu.VMEM((ROW_DEV // 256, 24, 256), F32),
            pltpu.VMEM((16, SLOTS), F32),
            pltpu.VMEM((ROW_DEV // 256, 256, SLOTS), BF),
            pltpu.VMEM((blocks, 16, 256), F32),
            pltpu.VMEM((2, 48, 256), F32),
            pltpu.VMEM((2, 48, 256), F32),
            pltpu.VMEM((blocks, NT_F * NP_F, 256), BF),
            pltpu.VMEM((NP_F * 16, 2 * C), F32),
            pltpu.VMEM((NP_F * 16, 2 * C), F32),
            pltpu.VMEM((C, NT_F * NP_F), BF),
            pltpu.VMEM((SLOTS, C), BF),
            pltpu.VMEM((N_BOX * SLOT, C), BF),
            pltpu.VMEM((ROW_DEV, C), BF),
            dma((P_DEV, 16)),
            dma((P_DEV, 16)),
            dma((P_DEV,)),
            dma((N_BOX,)),
            dma((N_BOX,)),
            dma((P_DEV, N_XY)),
            dma((P_DEV, N_XY)),
            dma((P_DEV,)),
            dma((P_DEV,)),
            dma((P_DEV, N_XY)),
            dma((P_DEV, N_XY)),
            dma((3, P_DEV)),
            dma((N_BOX,)),
            dma((N_BOX,)),
            dma,
            dma,
        ],
        compiler_params=pltpu.CompilerParams(
            collective_id=0, has_side_effects=True, vmem_limit_bytes=60 << 20
        ),
        name="step",
    )(
        pattern, tap_theta, tap_phi, weight_theta, weight_phi,
        jnp.asarray(theta_signs(), BF), jnp.asarray(phi_signs(), BF),
        row_box.reshape(1, ROW_DEV), row_offset, row_fwd, sines, cosines, quad,
    )


def per_device(*arrays):
    row_field, gradient = step(*arrays)
    return (row_field, gradient.reshape(ROW_DEV))


def solution(mesh):
    in_specs = (
        P("dir", "box", None, None),
        P(),
        P(),
        P(),
        P(),
        P(("dir", "box")),
        P(None, ("dir", "box")),
        P(("dir", "box"), None),
    )
    out_specs = (P(("dir", "box"), None), P(("dir", "box")))
    return jax.shard_map(
        per_device, mesh=mesh, in_specs=in_specs, out_specs=out_specs, check_vma=False
    )
```

time: 491 us -> 127 us (0.26)
  the two profiles are of different devices: /device:TPU:1 before, /device:TPU:6 now
where the time goes in v2:
time: 127 us
  Pallas kernels  117 us (92%)
  local copies, waits for them, and re-layouts  8.78 us (7%)
    pallas_call x1, Pallas kernels, step(): pl.pallas_call(step_kernel, out_shape=(jax.ShapeDtypeStruct((ROW_DEV, C),...  117 us
    unnamed x6, local copies, waits for them, and re-layouts  8.78 us

profile of v2, /device:TPU:6, one launch (start us, length us, event | category | flops | bytes accessed | tf_op | source)
XLA Modules:
  0.0 126.6 jit_solution(5833963931306366670)
XLA Ops:
  0.6 1.4 %copy.17.wt_t = bf16[64,12]{1,0:T(8,128)(2,1)} copy(bf16[64,12]{0,1:T(8,128)(2,1)} %param.16) | data formatting | bytes 3072 | tf_op args[3]
  2.0 1.4 %copy.15.tap_t = s32[64,12]{1,0:T(8,128)} copy(s32[64,12]{0,1:T(8,128)} %param.14) | data formatting | bytes 6144 | tf_op args[1]
  3.4 1.4 %copy.18.wt_p = bf16[128,12]{1,0:T(8,128)(2,1)} copy(bf16[128,12]{0,1:T(8,128)(2,1)} %param.17) | data formatting | bytes 6144 | tf_op args[4]
  4.8 1.4 %copy.16.tap_p = s32[128,12]{1,0:T(8,128)} copy(s32[128,12]{0,1:T(8,128)} %param.15) | data formatting | bytes 12288 | tf_op args[2]
  6.2 117.2 %step.1 = (bf16[2048,128]{1,0:T(8,128)(2,1)}, f32[1,2048]{1,0:T(1,128)}) custom-call(bf16[8,4,256,128]{3,2,1,0:T(8,128)(2,1)} %pat.1, s32[64,12]{1,0:T(8,128)} %copy.15.tap_t, s32[128,12]{1,0:T(8,128)} %copy.16.tap_p, bf16[64,12]{1,0:T(8,128)(2,1)} %copy.17.wt_t, bf16[128,12]{1,0:T(8,128)(2,1)} %copy.18.wt_p, bf16[32,32]{1,0:T(8,128)(2,1)} %constant.13.clone.sign_t, ...), custom_call_target="tpu_custom_call" | custom-call | tf_op jit(solution)/shard_map/step/pallas_call | solution.py:542
  123.4 1.9 %copy.21 = bf16[2048,128]{1,0:T(8,128)(2,1)} copy(bf16[2048,128]{1,0:T(8,128)(2,1)} %get-tuple-element.8) | data formatting | bytes 1048576
  125.3 1.3 %copy.22 = f32[2048]{0:T(1024)} copy(f32[2048]{0:T(1024)} %bitcast.3) | data formatting | bytes 16384

commit v3 on v2

--- a/solution.py
+++ b/solution.py
@@ -101,23 +101,23 @@
     return jnp.concatenate(parts, axis=0)
 
 
-def spread(taps, weights):
-    lane = lax.broadcasted_iota(jnp.int32, (taps.shape[0], 128), 1)
-    total = jnp.zeros(lane.shape, F32)
-    for j in range(taps.shape[1]):
+def spread(taps, weights, count):
+    sample = lax.broadcasted_iota(jnp.int32, (count, taps.shape[1]), 0)
+    total = jnp.zeros(sample.shape, F32)
+    for j in range(taps.shape[0]):
         total = total + jnp.where(
-            lane == taps[:, j : j + 1], weights[:, j : j + 1].astype(F32), 0.0
-        )
-    return total
+            sample == taps[j : j + 1, :], weights[j : j + 1, :].astype(F32), 0.0
+        )
+    return total.astype(BF)
 
 
 def step_kernel(
-    pat, tap_t, tap_p, wt_t, wt_p, sign_t, sign_p, box_of_row, off, fwd, sines, cosines, quad,
-    field, grad,
+    pat, tap_t, tap_p, wt_t, wt_p, sign_t, sign_p, box_of_row, off, sines, cosines, quad,
+    field,
     recv, ybuf, hbuf, twin, hsum, ry, rh, go, hotg, rg, mt, mp, geo, gacc, oh, gs, ex, ey, w,
-    acc_own, acc_hot, gt, f, r, fwd_v,
-    z_send, z_recv, z_self, g_send, g_recv, y_send, y_recv, t_send, t_recv, h_send, h_recv, self_sem,
-    r_send, r_recv, r_self, fwd_sem,
+    acc_own, acc_hot, gt, f, r, total, field_v,
+    z_send, z_recv, g_send, g_recv, y_send, y_recv, t_send, t_recv, h_send, h_recv,
+    r_send, r_recv, field_sem,
 ):
     d = lax.axis_index("dir")
     b = lax.axis_index("box")
@@ -140,7 +140,6 @@
 
     lax.fori_loop(1, 16, greet_z, 0)
     lax.fori_loop(1, N_BOX, greet_box, 0)
-    pl.semaphore_wait(barrier, 15 + N_BOX - 1)
 
 
     def z_copy(pi, k):
@@ -150,8 +149,8 @@
         return pltpu.make_async_remote_copy(
             src_ref=pat.at[:, pi, pl.ds(first, N_XY), :],
             dst_ref=recv.at[pi, zh, d],
-            send_sem=z_send.at[pi, k],
-            recv_sem=z_recv.at[pi, k],
+            send_sem=z_send.at[pi],
+            recv_sem=z_recv.at[pi],
             device_id=(d2, zh2 * N_XY + xy),
             device_id_type=MESH,
         )
@@ -159,7 +158,7 @@
     def z_own(pi):
         first = pl.multiple_of(d * N_BOX + zh * N_XY, N_XY)
         return pltpu.make_async_copy(
-            pat.at[:, pi, pl.ds(first, N_XY), :], recv.at[pi, zh, d], z_self.at[pi]
+            pat.at[:, pi, pl.ds(first, N_XY), :], recv.at[pi, zh, d], z_recv.at[pi]
         )
 
     def g_copy(k):
@@ -167,8 +166,8 @@
         return pltpu.make_async_remote_copy(
             src_ref=go.at[b2 // 2],
             dst_ref=rg.at[b],
-            send_sem=g_send.at[k],
-            recv_sem=g_recv.at[k],
+            send_sem=g_send,
+            recv_sem=g_recv,
             device_id=(d, b2),
             device_id_type=MESH,
         )
@@ -178,8 +177,8 @@
         return pltpu.make_async_remote_copy(
             src_ref=ybuf.at[pi, xy2],
             dst_ref=ry.at[pi, xy],
-            send_sem=y_send.at[pi, k],
-            recv_sem=y_recv.at[pi, k],
+            send_sem=y_send.at[pi],
+            recv_sem=y_recv.at[pi],
             device_id=(d, zh * N_XY + xy2),
             device_id_type=MESH,
         )
@@ -189,8 +188,8 @@
         return pltpu.make_async_remote_copy(
             src_ref=hsum.at[pi],
             dst_ref=rh.at[pi, xy],
-            send_sem=h_send.at[pi, k],
-            recv_sem=h_recv.at[pi, k],
+            send_sem=h_send.at[pi],
+            recv_sem=h_recv.at[pi],
             device_id=(d, zh * N_XY + xy2),
             device_id_type=MESH,
         )
@@ -206,52 +205,41 @@
         )
 
     def y_own(pi):
-        return pltpu.make_async_copy(ybuf.at[pi, xy], ry.at[pi, xy], self_sem.at[0, pi])
+        return pltpu.make_async_copy(ybuf.at[pi, xy], ry.at[pi, xy], y_recv.at[pi])
 
     def h_own(pi):
-        return pltpu.make_async_copy(hsum.at[pi], rh.at[pi, xy], self_sem.at[1, pi])
+        return pltpu.make_async_copy(hsum.at[pi], rh.at[pi, xy], h_recv.at[pi])
 
     def g_own():
-        return pltpu.make_async_copy(go.at[b // 2], rg.at[b], self_sem.at[2, 0])
+        return pltpu.make_async_copy(go.at[b // 2], rg.at[b], g_recv)
 
     def r_copy(b2):
         return pltpu.make_async_remote_copy(
             src_ref=f.at[pl.ds(pl.multiple_of(b2 * SLOT, SLOT), SLOT), :],
             dst_ref=r.at[pl.ds(pl.multiple_of(b * SLOT, SLOT), SLOT), :],
-            send_sem=r_send.at[b2],
-            recv_sem=r_recv.at[b],
+            send_sem=r_send,
+            recv_sem=r_recv.at[(zh + b2 // N_XY) % 2],
             device_id=(d, b2),
             device_id_type=MESH,
         )
 
-    def r_arrival(b2):
-        return pltpu.make_async_remote_copy(
-            src_ref=f.at[pl.ds(pl.multiple_of(b2 * SLOT, SLOT), SLOT), :],
-            dst_ref=r.at[pl.ds(pl.multiple_of(b2 * SLOT, SLOT), SLOT), :],
-            send_sem=r_send.at[b2],
-            recv_sem=r_recv.at[b2],
-            device_id=(d, b2),
-            device_id_type=MESH,
-        )
-
     def r_own():
         at = pl.ds(pl.multiple_of(b * SLOT, SLOT), SLOT)
-        return pltpu.make_async_copy(f.at[at, :], r.at[at, :], r_self)
-
-    def load_fwd():
-        return pltpu.make_async_copy(fwd, fwd_v, fwd_sem)
-
-    def each(n, copy, what):
+        return pltpu.make_async_copy(f.at[at, :], r.at[at, :], r_recv.at[0])
+
+    def each(n, copy):
         def one(k, carry):
-            getattr(copy(k), what)()
+            copy(k).start()
             return carry
 
         lax.fori_loop(1, n, one, 0)
 
-    for pi in range(P_DEV):
-        each(16, functools.partial(z_copy, pi), "start")
+    def wait_for(ref, sem):
+        pltpu.make_async_copy(ref, ref, sem).wait()
+
+    def z_start(pi):
+        each(16, functools.partial(z_copy, pi))
         z_own(pi).start()
-    load_fwd().start()
 
 
     box = box_of_row[...]
@@ -279,6 +267,9 @@
     hot_row = jnp.sum(onehot * is_hot, axis=0, keepdims=True)
     number = lax.broadcasted_iota(jnp.int32, (N_BOX, 1), 0).astype(F32)
     hot = jnp.sum(number * is_hot, axis=0, keepdims=True)
+    pl.semaphore_wait(barrier, 15 + N_BOX - 1)
+    z_start(0)
+
     pos = jnp.where(
         hot_row > 0.5, float(N_BOX * SLOT) + rank, dest.astype(F32) * float(SLOT) + rank
     )
@@ -296,20 +287,21 @@
 
     def sort_block(i, carry):
         hits = one_hot(geo[i, 16:17], lane128)
-        oh[i] = hits
+        oh[pl.ds(pl.multiple_of(i * width, width), width), :] = hits
         gacc[...] += jnp.dot(geo[i, :16].astype(BF), hits, preferred_element_type=F32)
         return carry
 
     lax.fori_loop(0, ROW_DEV // width, sort_block, 0)
     for m in range(N_BOX // 2):
-        go[m] = gacc[:, m * 128 : (m + 1) * 128].astype(BF)
+        go[m] = gacc[:4, m * 128 : (m + 1) * 128].astype(BF)
     for m in range(2):
-        hotg[m] = gacc[:, N_BOX * SLOT + m * 128 : N_BOX * SLOT + (m + 1) * 128]
-    each(N_BOX, g_copy, "start")
+        hotg[m] = gacc[:8, N_BOX * SLOT + m * 128 : N_BOX * SLOT + (m + 1) * 128]
+    each(N_BOX, g_copy)
     g_own().start()
-
-
-    a_theta = spread(tap_t[...], wt_t[...]).T[:NT_F].astype(BF)
+    z_start(1)
+
+
+    a_theta = spread(tap_t[...], wt_t[...], NT_F)
     ah = jnp.dot(sign_t[...], a_theta, preferred_element_type=F32).astype(BF)
     col = lax.broadcasted_iota(jnp.int32, (NT, NT * N_XY), 1)
     row = lax.broadcasted_iota(jnp.int32, (NT, NT * N_XY), 0)
@@ -321,7 +313,7 @@
     local = hot - (zh * N_XY).astype(F32)
     mt[N_XY * NT_F :, :] = jnp.where(lane_g.astype(F32) == local, v, 0.0).astype(BF)
 
-    a_phi = spread(tap_p[...], wt_p[...]).T[:NP_F].astype(BF)
+    a_phi = spread(tap_p[...], wt_p[...], NP_F)
     bh = jnp.dot(sign_p[...], a_phi, preferred_element_type=F32).astype(BF)
     col = lax.broadcasted_iota(jnp.int32, (NP, NP * 16), 1) // 16
     row = lax.broadcasted_iota(jnp.int32, (NP, NP * 16), 0)
@@ -340,8 +332,7 @@
     low = lane < HALF
 
     def gather_geometry():
-        g_own().wait()
-        each(N_BOX, g_copy, "wait_recv")
+        wait_for(rg, g_recv)
         odd = b % 2 == 1
 
         def side(m):
@@ -350,7 +341,7 @@
 
         for m in range(N_BOX // 2):
             second = pltpu.roll(side(2 * m + 1), HALF, 1)
-            gs[m // 2, :, m % 2 * 128 : (m % 2 + 1) * 128] = jnp.where(low, side(2 * m), second)
+            gs[m // 2, :4, m % 2 * 128 : (m % 2 + 1) * 128] = jnp.where(low[:4], side(2 * m), second)
         for m in range(2):
             gs[N_BOX // 4, :, m * 128 : (m + 1) * 128] = hotg[m]
 
@@ -398,8 +389,7 @@
 
 
     def theta_step(pi):
-        z_own(pi).wait()
-        each(16, functools.partial(z_copy, pi), "wait_recv")
+        wait_for(recv.at[pi], z_recv.at[pi])
         x = jnp.concatenate(
             [recv[pi, 0].reshape(NT * N_XY, C), recv[pi, 1].reshape(NT * N_XY, C)], axis=1
         )
@@ -408,19 +398,18 @@
             part = y[:, z * C : (z + 1) * C]
             ybuf[pi, :, z] = part[: N_XY * NT_F].reshape(N_XY, NT_F, C)
             hbuf[pi, z] = part[N_XY * NT_F :]
-        each(N_XY, functools.partial(y_copy, pi), "start")
+        each(N_XY, functools.partial(y_copy, pi))
         t_copy(pi).start()
         y_own(pi).start()
 
     def hot_step(pi):
         t_copy(pi).wait_recv()
         hsum[pi] = hbuf[pi] + twin[pi]
-        each(N_XY, functools.partial(h_copy, pi), "start")
+        each(N_XY, functools.partial(h_copy, pi))
         h_own(pi).start()
 
-    def phi_step(pi, part, own, copy, acc):
-        own(pi).wait()
-        each(N_XY, functools.partial(copy, pi), "wait_recv")
+    def phi_step(pi, part, sem, acc):
+        wait_for(part.at[pi], sem.at[pi])
         x = jnp.concatenate(
             [part[pi, :, :, c * 16 : (c + 1) * 16, :].reshape(512, C) for c in range(2)], axis=1
         )
@@ -451,7 +440,7 @@
         return jnp.dot(gt[...], w[i], preferred_element_type=F32).T.astype(BF)
 
     def send_block(i, carry):
-        at = (b // 4 + i) % (N_BOX // 4)
+        at = (1 - zh + i // 4) % 2 * 4 + (b // 4 + i) % 4
         f[pl.ds(pl.multiple_of(at * 256, 256), 256), :] = field_block(at)
         for j in range(4):
             b2 = at * 4 + j
@@ -466,68 +455,76 @@
 
         return carry
 
-    own_args = (ry, y_own, y_copy, acc_own)
-    hot_args = (rh, h_own, h_copy, acc_hot)
+    own_args = (ry, y_recv, acc_own)
+    hot_args = (rh, h_recv, acc_hot)
     theta_step(0)
+    z_start(2)
     gather_geometry()
-    lax.fori_loop(0, 3, phases, 0)
+    lax.fori_loop(0, 4, phases, 0)
+    theta_step(1)
+    z_start(3)
     hot_step(0)
-    theta_step(1)
     phi_step(0, *own_args)
-    lax.fori_loop(3, 6, phases, 0)
+    lax.fori_loop(4, 9, phases, 0)
+    theta_step(2)
     hot_step(1)
-    theta_step(2)
     phi_step(1, *own_args)
     phi_step(0, *hot_args)
-    lax.fori_loop(6, 9, phases, 0)
+    theta_step(3)
     hot_step(2)
-    theta_step(3)
     phi_step(2, *own_args)
     phi_step(1, *hot_args)
+    phi_step(3, *own_args)
     hot_step(3)
-    phi_step(3, *own_args)
     directions(acc_own)
     lax.fori_loop(0, N_BOX // 4, send_block, 0)
     phi_step(2, *hot_args)
+    for pi in range(P_DEV):
+        wait_for(f.at[: 15 * 128], z_send.at[pi])
+        wait_for(f.at[: 15 * SLOT], y_send.at[pi])
+    wait_for(rg.at[: N_BOX - 1], g_send)
     phi_step(3, *hot_args)
     directions(acc_hot)
     f[N_BOX * SLOT :, :] = field_block(N_BOX // 4)
-    load_fwd().wait()
-    r_own().wait()
-
-    def arrived(k, carry):
-        r_arrival((b + k) % N_BOX).wait_recv()
+
+    half = N_BOX * SLOT // 2
+    here = pl.multiple_of(zh * half, half)
+    there = pl.multiple_of(half - zh * half, half)
+    wait_for(r.at[pl.ds(here, half), :], r_recv.at[0])
+
+    def place_here(i, carry):
+        at = pl.multiple_of(i * 1024, 1024)
+        v = jnp.dot(
+            oh[pl.ds(at, 1024), pl.ds(here, half)],
+            r[pl.ds(here, half), :],
+            preferred_element_type=F32,
+        )
+        total[pl.ds(at, 1024), :] = v + jnp.dot(
+            oh[pl.ds(at, 1024), N_BOX * SLOT :],
+            f[N_BOX * SLOT :, :],
+            preferred_element_type=F32,
+        )
         return carry
 
-    lax.fori_loop(1, N_BOX, arrived, 0)
-
-    def place(i, carry):
-        hits = oh[i]
-        v = jnp.dot(hits[:, : N_BOX * SLOT], r[...], preferred_element_type=F32)
-        v = v + jnp.dot(hits[:, N_BOX * SLOT :], f[N_BOX * SLOT :, :], preferred_element_type=F32)
-        v = v.astype(BF)
-        at = pl.multiple_of(i * 256, 256)
-        field[pl.ds(at, 256), :] = v
-        product = fwd_v[pl.ds(at, 256), :].astype(F32) * v.astype(F32)
-        grad[:, pl.ds(at, 256)] = jnp.sum(product.T, axis=0, keepdims=True) * (0.5 / math.sqrt(C))
-        return carry
-
-    lax.fori_loop(0, ROW_DEV // 256, place, 0)
-    each(N_BOX, g_copy, "wait_send")
+    lax.fori_loop(0, ROW_DEV // 1024, place_here, 0)
     for pi in range(P_DEV):
         t_copy(pi).wait_send()
-        each(16, functools.partial(z_copy, pi), "wait_send")
-        each(N_XY, functools.partial(y_copy, pi), "wait_send")
-        each(N_XY, functools.partial(h_copy, pi), "wait_send")
-
-    def sent(k, carry):
-        r_copy((b + k) % N_BOX).wait_send()
-        return carry
-
-    lax.fori_loop(1, N_BOX, sent, 0)
-
-
-def step(pattern, tap_theta, tap_phi, weight_theta, weight_phi, row_box, row_offset, row_fwd):
+        wait_for(f.at[: 15 * SLOT], h_send.at[pi])
+    wait_for(f.at[: 31 * SLOT], r_send)
+    wait_for(r.at[pl.ds(there, half), :], r_recv.at[1])
+    for i in range(2):
+        at = pl.ds(i * 1024, 1024)
+        v = total[at, :] + jnp.dot(
+            oh[at, pl.ds(there, half)], r[pl.ds(there, half), :], preferred_element_type=F32
+        )
+        field_v[at, :] = v.astype(BF)
+        pltpu.make_async_copy(field_v.at[at, :], field.at[at, :], field_sem.at[i]).start()
+    for i in range(2):
+        at = pl.ds(i * 1024, 1024)
+        pltpu.make_async_copy(field_v.at[at, :], field.at[at, :], field_sem.at[i]).wait()
+
+
+def step(pattern, tap_theta, tap_phi, weight_theta, weight_phi, row_box, row_offset):
     n = np.arange(NT_F) + 0.5
     wide = lambda v: jnp.asarray(np.repeat(v[:, None], 256, axis=1), F32)
     sines = wide(np.sin(np.pi * n / NT_F))
@@ -541,12 +538,9 @@
     blocks = SLOTS // 256
     return pl.pallas_call(
         step_kernel,
-        out_shape=(
-            jax.ShapeDtypeStruct((ROW_DEV, C), BF),
-            jax.ShapeDtypeStruct((1, ROW_DEV), F32),
-        ),
-        in_specs=[anywhere] + [vm] * 8 + [anywhere] + [vm] * 3,
-        out_specs=(vm, vm),
+        out_shape=jax.ShapeDtypeStruct((ROW_DEV, C), BF),
+        in_specs=[anywhere] + [vm] * 11,
+        out_specs=anywhere,
         scratch_shapes=[
             pltpu.VMEM((P_DEV, 2, N_DIR, T_DEV, N_XY, C), BF),
             pltpu.VMEM(theta, BF),
@@ -555,15 +549,15 @@
             pltpu.VMEM(hot, BF),
             pltpu.VMEM(theta, BF),
             pltpu.VMEM(theta, BF),
-            pltpu.VMEM((N_BOX // 2, 16, 128), BF),
-            pltpu.VMEM((2, 16, 128), F32),
-            pltpu.VMEM((N_BOX, 16, 128), BF),
+            pltpu.VMEM((N_BOX // 2, 4, 128), BF),
+            pltpu.VMEM((2, 8, 128), F32),
+            pltpu.VMEM((N_BOX, 4, 128), BF),
             pltpu.VMEM((N_XY * NT_F + NT_F, NT * N_XY), BF),
             pltpu.VMEM((NP_F * 16, NP * 16), BF),
             pltpu.VMEM((ROW_DEV // 256, 24, 256), F32),
             pltpu.VMEM((16, SLOTS), F32),
-            pltpu.VMEM((ROW_DEV // 256, 256, SLOTS), BF),
-            pltpu.VMEM((blocks, 16, 256), F32),
+            pltpu.VMEM((ROW_DEV, SLOTS), BF),
+            pltpu.VMEM((blocks, 8, 256), F32),
             pltpu.VMEM((2, 48, 256), F32),
             pltpu.VMEM((2, 48, 256), F32),
             pltpu.VMEM((blocks, NT_F * NP_F, 256), BF),
@@ -572,38 +566,59 @@
             pltpu.VMEM((C, NT_F * NP_F), BF),
             pltpu.VMEM((SLOTS, C), BF),
             pltpu.VMEM((N_BOX * SLOT, C), BF),
+            pltpu.VMEM((ROW_DEV, C), F32),
             pltpu.VMEM((ROW_DEV, C), BF),
-            dma((P_DEV, 16)),
-            dma((P_DEV, 16)),
-            dma((P_DEV,)),
-            dma((N_BOX,)),
-            dma((N_BOX,)),
-            dma((P_DEV, N_XY)),
-            dma((P_DEV, N_XY)),
-            dma((P_DEV,)),
-            dma((P_DEV,)),
-            dma((P_DEV, N_XY)),
-            dma((P_DEV, N_XY)),
-            dma((3, P_DEV)),
-            dma((N_BOX,)),
-            dma((N_BOX,)),
+            dma((P_DEV,)),
+            dma((P_DEV,)),
             dma,
             dma,
+            dma((P_DEV,)),
+            dma((P_DEV,)),
+            dma((P_DEV,)),
+            dma((P_DEV,)),
+            dma((P_DEV,)),
+            dma((P_DEV,)),
+            dma,
+            dma((2,)),
+            dma((2,)),
         ],
         compiler_params=pltpu.CompilerParams(
             collective_id=0, has_side_effects=True, vmem_limit_bytes=60 << 20
         ),
         name="step",
     )(
-        pattern, tap_theta, tap_phi, weight_theta, weight_phi,
+        pattern, tap_theta.T, tap_phi.T, weight_theta.T, weight_phi.T,
         jnp.asarray(theta_signs(), BF), jnp.asarray(phi_signs(), BF),
-        row_box.reshape(1, ROW_DEV), row_offset, row_fwd, sines, cosines, quad,
+        row_box.reshape(1, ROW_DEV), row_offset, sines, cosines, quad,
     )
 
 
+def finish_kernel(field, fwd, out, grad):
+    v = field[...]
+    out[...] = v
+    product = fwd[...].astype(F32) * v.astype(F32)
+    grad[...] = (jnp.sum(product.T, axis=0, keepdims=True) * (0.5 / math.sqrt(C))).reshape(grad.shape)
+
+
+def finish(field, fwd):
+    rows = 1024
+    block = pl.BlockSpec((rows, C), lambda i: (i, 0))
+    return pl.pallas_call(
+        finish_kernel,
+        out_shape=(
+            jax.ShapeDtypeStruct((ROW_DEV, C), BF),
+            jax.ShapeDtypeStruct((ROW_DEV,), F32),
+        ),
+        grid=(ROW_DEV // rows,),
+        in_specs=[block, block],
+        out_specs=(block, pl.BlockSpec((rows,), lambda i: (i,))),
+        name="finish",
+    )(field, fwd)
+
+
 def per_device(*arrays):
-    row_field, gradient = step(*arrays)
-    return (row_field, gradient.reshape(ROW_DEV))
+    field = step(*arrays[:-1])
+    return finish(field, arrays[-1])
 
 
 def solution(mesh):

time: 127 us -> 91.5 us (0.72)
  the two profiles are of different devices: /device:TPU:6 before, /device:TPU:32 now
where the time goes in v3:
time: 91.5 us; the launch traced here: 91.3 us
  Pallas kernels  90.6 us (99%)
    pallas_call x1, Pallas kernels, step(): pl.pallas_call(step_kernel, out_shape=jax.ShapeDtypeStruct((ROW_DEV, C),...  88.5 us
    pallas_call x1, Pallas kernels, finish(): pl.pallas_call(finish_kernel, out_shape=(jax.ShapeDtypeStruct((ROW_DEV, C...  2.1 us

profile of v3, /device:TPU:32, one launch (start us, length us, event | category | flops | bytes accessed | tf_op | source)
XLA Modules:
  0.0 91.3 jit_solution(16632920088637192406)
XLA Ops:
  0.6 88.5 %step.1.field = bf16[2048,128]{1,0:T(8,128)(2,1)} custom-call(bf16[8,4,256,128]{3,2,1,0:T(8,128)(2,1)} %pat.1, s32[12,64]{1,0:T(8,128)} %bitcast.5, s32[12,128]{1,0:T(8,128)} %bitcast.6, bf16[12,64]{1,0:T(8,128)(2,1)} %bitcast.8, bf16[12,128]{1,0:T(8,128)(2,1)} %bitcast.9, bf16[32,32]{1,0:T(8,128)(2,1)} %constant.13.clone.sign_t, ...), custom_call_target="tpu_custom_call" | custom-call | tf_op jit(solution)/shard_map/step/pallas_call | solution.py:539
  89.2 2.1 %finish.1 = (bf16[2048,128]{1,0:T(8,128)(2,1)}, f32[2048]{0:T(1024)}) custom-call(bf16[2048,128]{1,0:T(8,128)(2,1)} %step.1.field, bf16[2048,128]{1,0:T(8,128)(2,1)} %fwd.1), custom_call_target="tpu_custom_call" | custom-call | tf_op jit(solution)/shard_map/finish/pallas_call | solution.py:606

commit v4 on v3

--- a/solution.py
+++ b/solution.py
@@ -24,6 +24,8 @@
 SLOTS = N_BOX * SLOT + HOT
 P_DEV = NP // N_BOX
 T_DEV = NT // N_DIR
+LAST = P_DEV - 1
+SMALL = 11
 
 box_phase = 50.265482
 
@@ -111,14 +113,16 @@
     return total.astype(BF)
 
 
-def step_kernel(
-    pat, tap_t, tap_p, wt_t, wt_p, sign_t, sign_p, box_of_row, off, sines, cosines, quad,
-    field,
-    recv, ybuf, hbuf, twin, hsum, ry, rh, go, hotg, rg, mt, mp, geo, gacc, oh, gs, ex, ey, w,
-    acc_own, acc_hot, gt, f, r, total, field_v,
-    z_send, z_recv, g_send, g_recv, y_send, y_recv, t_send, t_recv, h_send, h_recv,
-    r_send, r_recv, field_sem,
-):
+def step_kernel(pat, *refs):
+    small, refs = refs[:SMALL], refs[SMALL:]
+    (
+        field, recv, ybuf, hbuf, twin, hsum, ry, rh, go, hotg, rg, mt, mp, geo, gacc, oh, gs, ex, ey, w,
+        acc_own, acc_hot, gt, f, r, total, field_v,
+        z_send, z_recv, g_send, g_recv, y_send, y_recv, t_send, t_recv, h_send, h_recv,
+        r_send, r_recv, field_sem, small_sem,
+    ) = refs[: len(refs) - SMALL]
+    held = refs[len(refs) - SMALL :]
+    tap_t, tap_p, wt_t, wt_p, sign_t, sign_p, box_of_row, off, sines, cosines, quad = held
     d = lax.axis_index("dir")
     b = lax.axis_index("box")
     zh = b // N_XY
@@ -155,10 +159,10 @@
             device_id_type=MESH,
         )
 
-    def z_own(pi):
+    def z_own(pi, half=0):
         first = pl.multiple_of(d * N_BOX + zh * N_XY, N_XY)
         return pltpu.make_async_copy(
-            pat.at[:, pi, pl.ds(first, N_XY), :], recv.at[pi, zh, d], z_recv.at[pi]
+            pat.at[:, pi, pl.ds(first, N_XY), :], recv.at[pi, zh, d], z_recv.at[pi + half]
         )
 
     def g_copy(k):
@@ -218,7 +222,7 @@
             src_ref=f.at[pl.ds(pl.multiple_of(b2 * SLOT, SLOT), SLOT), :],
             dst_ref=r.at[pl.ds(pl.multiple_of(b * SLOT, SLOT), SLOT), :],
             send_sem=r_send,
-            recv_sem=r_recv.at[(zh + b2 // N_XY) % 2],
+            recv_sem=r_recv.at[(zh + b2 // N_XY) % 2 * (1 + (b2 // 4 + 8 - b // 4) % 4)],
             device_id=(d, b2),
             device_id_type=MESH,
         )
@@ -237,9 +241,59 @@
     def wait_for(ref, sem):
         pltpu.make_async_copy(ref, ref, sem).wait()
 
+    def z_half_copy(zh2, j):
+        d2 = (d + j) % N_DIR
+        first = pl.multiple_of(d2 * N_BOX + zh2 * N_XY, N_XY)
+        return pltpu.make_async_remote_copy(
+            src_ref=pat.at[:, LAST, pl.ds(first, N_XY), :],
+            dst_ref=recv.at[LAST, zh, d],
+            send_sem=z_send.at[LAST],
+            recv_sem=z_recv.at[LAST + (zh + zh2 + 1) % 2],
+            device_id=(d2, zh2 * N_XY + xy),
+            device_id_type=MESH,
+        )
+
+    def z_start_last():
+        def other(j, carry):
+            z_half_copy(1 - zh, j).start()
+            return carry
+
+        lax.fori_loop(0, N_DIR, other, 0)
+        each(N_DIR, functools.partial(z_half_copy, zh))
+        z_own(LAST, 1).start()
+
+    def y_half_copy(half, sem, k):
+        xy2 = (xy + k) % N_XY
+        return pltpu.make_async_remote_copy(
+            src_ref=ybuf.at[LAST, xy2, half],
+            dst_ref=ry.at[LAST, xy, half],
+            send_sem=y_send.at[LAST],
+            recv_sem=y_recv.at[sem],
+            device_id=(d, zh * N_XY + xy2),
+            device_id_type=MESH,
+        )
+
+    def theta_half(half, sem):
+        wait_for(recv.at[LAST, half], z_recv.at[sem])
+        x = recv[LAST, half].reshape(NT * N_XY, C)
+        y = jnp.dot(mt[...], x, preferred_element_type=F32).astype(BF)
+        ybuf[LAST, :, half] = y[: N_XY * NT_F].reshape(N_XY, NT_F, C)
+        hbuf[LAST, half] = y[N_XY * NT_F :]
+        each(N_XY, functools.partial(y_half_copy, half, sem))
+        pltpu.make_async_copy(
+            ybuf.at[LAST, xy, half], ry.at[LAST, xy, half], y_recv.at[sem]
+        ).start()
+
     def z_start(pi):
         each(16, functools.partial(z_copy, pi))
         z_own(pi).start()
+
+    for i in range(SMALL):
+        pltpu.make_async_copy(small[i], held[i], small_sem.at[i]).start()
+    pl.semaphore_wait(barrier, 15 + N_BOX - 1)
+    z_start(0)
+    for i in range(SMALL):
+        pltpu.make_async_copy(small[i], held[i], small_sem.at[i]).wait()
 
 
     box = box_of_row[...]
@@ -267,8 +321,6 @@
     hot_row = jnp.sum(onehot * is_hot, axis=0, keepdims=True)
     number = lax.broadcasted_iota(jnp.int32, (N_BOX, 1), 0).astype(F32)
     hot = jnp.sum(number * is_hot, axis=0, keepdims=True)
-    pl.semaphore_wait(barrier, 15 + N_BOX - 1)
-    z_start(0)
 
     pos = jnp.where(
         hot_row > 0.5, float(N_BOX * SLOT) + rank, dest.astype(F32) * float(SLOT) + rank
@@ -399,8 +451,9 @@
             ybuf[pi, :, z] = part[: N_XY * NT_F].reshape(N_XY, NT_F, C)
             hbuf[pi, z] = part[N_XY * NT_F :]
         each(N_XY, functools.partial(y_copy, pi))
-        t_copy(pi).start()
         y_own(pi).start()
+        if pi < 2:
+            t_copy(pi).start()
 
     def hot_step(pi):
         t_copy(pi).wait_recv()
@@ -409,7 +462,8 @@
         h_own(pi).start()
 
     def phi_step(pi, part, sem, acc):
-        wait_for(part.at[pi], sem.at[pi])
+        bytes_of = part.at[pi, : N_XY // 2] if part is ry and pi == LAST else part.at[pi]
+        wait_for(bytes_of, sem.at[pi])
         x = jnp.concatenate(
             [part[pi, :, :, c * 16 : (c + 1) * 16, :].reshape(512, C) for c in range(2)], axis=1
         )
@@ -462,7 +516,7 @@
     gather_geometry()
     lax.fori_loop(0, 4, phases, 0)
     theta_step(1)
-    z_start(3)
+    z_start_last()
     hot_step(0)
     phi_step(0, *own_args)
     lax.fori_loop(4, 9, phases, 0)
@@ -470,11 +524,15 @@
     hot_step(1)
     phi_step(1, *own_args)
     phi_step(0, *hot_args)
-    theta_step(3)
+    theta_half(1 - zh, LAST)
+    phi_step(2, *own_args)
+    theta_half(zh, LAST + 1)
+    t_copy(2).start()
+    t_copy(3).start()
+    phi_step(1, *hot_args)
+    wait_for(ry.at[LAST, : N_XY // 2], y_recv.at[LAST + 1])
+    phi_step(3, *own_args)
     hot_step(2)
-    phi_step(2, *own_args)
-    phi_step(1, *hot_args)
-    phi_step(3, *own_args)
     hot_step(3)
     directions(acc_own)
     lax.fori_loop(0, N_BOX // 4, send_block, 0)
@@ -511,14 +569,18 @@
         t_copy(pi).wait_send()
         wait_for(f.at[: 15 * SLOT], h_send.at[pi])
     wait_for(f.at[: 31 * SLOT], r_send)
-    wait_for(r.at[pl.ds(there, half), :], r_recv.at[1])
-    for i in range(2):
-        at = pl.ds(i * 1024, 1024)
-        v = total[at, :] + jnp.dot(
-            oh[at, pl.ds(there, half)], r[pl.ds(there, half), :], preferred_element_type=F32
-        )
-        field_v[at, :] = v.astype(BF)
-        pltpu.make_async_copy(field_v.at[at, :], field.at[at, :], field_sem.at[i]).start()
+    for piece in range(4):
+        source = (b // 4 + 4 - piece) % 4
+        lanes = pl.ds(pl.multiple_of(there + source * 256, 256), 256)
+        wait_for(r.at[lanes, :], r_recv.at[1 + piece])
+        for i in range(2):
+            at = pl.ds(i * 1024, 1024)
+            v = total[at, :] + jnp.dot(oh[at, lanes], r[lanes, :], preferred_element_type=F32)
+            if piece < 3:
+                total[at, :] = v
+            else:
+                field_v[at, :] = v.astype(BF)
+                pltpu.make_async_copy(field_v.at[at, :], field.at[at, :], field_sem.at[i]).start()
     for i in range(2):
         at = pl.ds(i * 1024, 1024)
         pltpu.make_async_copy(field_v.at[at, :], field.at[at, :], field_sem.at[i]).wait()
@@ -530,7 +592,11 @@
     sines = wide(np.sin(np.pi * n / NT_F))
     cosines = wide(np.cos(np.pi * n / NT_F))
     quad = wide(np.sin(np.pi * n[:16] / NT_F) * math.sqrt(2.0 / (NT_F * NP_F)))[:, :C]
-    vm = pl.BlockSpec(memory_space=pltpu.VMEM)
+    small = (
+        tap_theta.T, tap_phi.T, weight_theta.T, weight_phi.T,
+        jnp.asarray(theta_signs(), BF), jnp.asarray(phi_signs(), BF),
+        row_box.reshape(1, ROW_DEV), row_offset, sines, cosines, quad,
+    )
     anywhere = pl.BlockSpec(memory_space=pl.ANY)
     dma = pltpu.SemaphoreType.DMA
     theta = (P_DEV, N_XY, 2, NT_F, C)
@@ -539,7 +605,7 @@
     return pl.pallas_call(
         step_kernel,
         out_shape=jax.ShapeDtypeStruct((ROW_DEV, C), BF),
-        in_specs=[anywhere] + [vm] * 11,
+        in_specs=[anywhere] * (1 + SMALL),
         out_specs=anywhere,
         scratch_shapes=[
             pltpu.VMEM((P_DEV, 2, N_DIR, T_DEV, N_XY, C), BF),
@@ -569,28 +635,26 @@
             pltpu.VMEM((ROW_DEV, C), F32),
             pltpu.VMEM((ROW_DEV, C), BF),
             dma((P_DEV,)),
-            dma((P_DEV,)),
+            dma((P_DEV + 1,)),
             dma,
             dma,
             dma((P_DEV,)),
-            dma((P_DEV,)),
+            dma((P_DEV + 1,)),
             dma((P_DEV,)),
             dma((P_DEV,)),
             dma((P_DEV,)),
             dma((P_DEV,)),
             dma,
+            dma((5,)),
             dma((2,)),
-            dma((2,)),
-        ],
+            dma((SMALL,)),
+        ]
+        + [pltpu.VMEM(v.shape, v.dtype) for v in small],
         compiler_params=pltpu.CompilerParams(
             collective_id=0, has_side_effects=True, vmem_limit_bytes=60 << 20
         ),
         name="step",
-    )(
-        pattern, tap_theta.T, tap_phi.T, weight_theta.T, weight_phi.T,
-        jnp.asarray(theta_signs(), BF), jnp.asarray(phi_signs(), BF),
-        row_box.reshape(1, ROW_DEV), row_offset, sines, cosines, quad,
-    )
+    )(pattern, *small)
 
 
 def finish_kernel(field, fwd, out, grad):

time: 91.5 us -> 89.4 us (0.977)
  Pallas kernels: 90.6 us -> 88 us
    pallas_call x1, Pallas kernels: 88.5 us -> 85.9 us  [step(): pl.pallas_call(step_kernel, out_shape=jax.ShapeDtypeStruct((ROW_DEV, C),...]
where the time goes in v4:
time: 89.4 us; the launch traced here: 88.7 us
  Pallas kernels  88 us (98%)
    pallas_call x1, Pallas kernels, step(): pl.pallas_call(step_kernel, out_shape=jax.ShapeDtypeStruct((ROW_DEV, C),...  85.9 us
    pallas_call x1, Pallas kernels, finish(): pl.pallas_call(finish_kernel, out_shape=(jax.ShapeDtypeStruct((ROW_DEV, C...  2.1 us

profile of v4, /device:TPU:32, one launch (start us, length us, event | category | flops | bytes accessed | tf_op | source)
XLA Modules:
  0.0 88.7 jit_solution(9351270841564091886)
XLA Ops:
  0.6 85.9 %step.1.field = bf16[2048,128]{1,0:T(8,128)(2,1)} custom-call(bf16[8,4,256,128]{3,2,1,0:T(8,128)(2,1)} %pat.1, s32[12,64]{1,0:T(8,128)} %bitcast.5, s32[12,128]{1,0:T(8,128)} %bitcast.6, bf16[12,64]{1,0:T(8,128)(2,1)} %bitcast.8, bf16[12,128]{1,0:T(8,128)(2,1)} %bitcast.9, bf16[32,32]{1,0:T(8,128)(2,1)} %constant.13.clone.refs_4_, ...), custom_call_target="tpu_custom_call" | custom-call | tf_op jit(solution)/shard_map/step/pallas_call | solution.py:605
  86.6 2.1 %finish.1 = (bf16[2048,128]{1,0:T(8,128)(2,1)}, f32[2048]{0:T(1024)}) custom-call(bf16[2048,128]{1,0:T(8,128)(2,1)} %step.1.field, bf16[2048,128]{1,0:T(8,128)(2,1)} %fwd.1), custom_call_target="tpu_custom_call" | custom-call | tf_op jit(solution)/shard_map/finish/pallas_call | solution.py:670

commit v5 on v4

--- a/solution.py
+++ b/solution.py
@@ -222,7 +222,7 @@
             src_ref=f.at[pl.ds(pl.multiple_of(b2 * SLOT, SLOT), SLOT), :],
             dst_ref=r.at[pl.ds(pl.multiple_of(b * SLOT, SLOT), SLOT), :],
             send_sem=r_send,
-            recv_sem=r_recv.at[(zh + b2 // N_XY) % 2 * (1 + (b2 // 4 + 8 - b // 4) % 4)],
+            recv_sem=r_recv.at[(zh + b2 // N_XY) % 2 * (1 + (b2 // 4 + 8 - b // 4) % 4 // 2)],
             device_id=(d, b2),
             device_id_type=MESH,
         )
@@ -530,9 +530,9 @@
     t_copy(2).start()
     t_copy(3).start()
     phi_step(1, *hot_args)
+    hot_step(2)
     wait_for(ry.at[LAST, : N_XY // 2], y_recv.at[LAST + 1])
     phi_step(3, *own_args)
-    hot_step(2)
     hot_step(3)
     directions(acc_own)
     lax.fori_loop(0, N_BOX // 4, send_block, 0)
@@ -569,20 +569,24 @@
         t_copy(pi).wait_send()
         wait_for(f.at[: 15 * SLOT], h_send.at[pi])
     wait_for(f.at[: 31 * SLOT], r_send)
-    for piece in range(4):
-        source = (b // 4 + 4 - piece) % 4
-        lanes = pl.ds(pl.multiple_of(there + source * 256, 256), 256)
-        wait_for(r.at[lanes, :], r_recv.at[1 + piece])
-        for i in range(2):
-            at = pl.ds(i * 1024, 1024)
-            v = total[at, :] + jnp.dot(oh[at, lanes], r[lanes, :], preferred_element_type=F32)
-            if piece < 3:
+    for piece in range(2):
+        lanes = []
+        for k in range(2):
+            source = (b // 4 + 4 - 2 * piece - k) % 4
+            lanes.append(pl.ds(pl.multiple_of(there + source * 256, 256), 256))
+        wait_for(f.at[:512, :], r_recv.at[1 + piece])
+        part = jnp.concatenate([r[k, :] for k in lanes], axis=0)
+        for i in range(4):
+            at = pl.ds(i * 512, 512)
+            hits = jnp.concatenate([oh[at, k] for k in lanes], axis=1)
+            v = total[at, :] + jnp.dot(hits, part, preferred_element_type=F32)
+            if piece == 0:
                 total[at, :] = v
             else:
                 field_v[at, :] = v.astype(BF)
                 pltpu.make_async_copy(field_v.at[at, :], field.at[at, :], field_sem.at[i]).start()
-    for i in range(2):
-        at = pl.ds(i * 1024, 1024)
+    for i in range(4):
+        at = pl.ds(i * 512, 512)
         pltpu.make_async_copy(field_v.at[at, :], field.at[at, :], field_sem.at[i]).wait()
 
 
@@ -645,8 +649,8 @@
             dma((P_DEV,)),
             dma((P_DEV,)),
             dma,
-            dma((5,)),
-            dma((2,)),
+            dma((3,)),
+            dma((4,)),
             dma((SMALL,)),
         ]
         + [pltpu.VMEM(v.shape, v.dtype) for v in small],

time: 89.4 us -> 88.6 us (level)
  no operation moved by 1% of the time
where the time goes in v5:
time: 88.6 us; the launch traced here: 88.5 us
  Pallas kernels  87.9 us (99%)
    pallas_call x1, Pallas kernels, step(): pl.pallas_call(step_kernel, out_shape=jax.ShapeDtypeStruct((ROW_DEV, C),...  85.8 us
    pallas_call x1, Pallas kernels, finish(): pl.pallas_call(finish_kernel, out_shape=(jax.ShapeDtypeStruct((ROW_DEV, C...  2.1 us

profile of v5, /device:TPU:32, one launch (start us, length us, event | category | flops | bytes accessed | tf_op | source)
XLA Modules:
  0.0 88.5 jit_solution(14242347482329529536)
XLA Ops:
  0.6 85.8 %step.1.field = bf16[2048,128]{1,0:T(8,128)(2,1)} custom-call(bf16[8,4,256,128]{3,2,1,0:T(8,128)(2,1)} %pat.1, s32[12,64]{1,0:T(8,128)} %bitcast.5, s32[12,128]{1,0:T(8,128)} %bitcast.6, bf16[12,64]{1,0:T(8,128)(2,1)} %bitcast.8, bf16[12,128]{1,0:T(8,128)(2,1)} %bitcast.9, bf16[32,32]{1,0:T(8,128)(2,1)} %constant.13.clone.refs_4_, ...), custom_call_target="tpu_custom_call" | custom-call | tf_op jit(solution)/shard_map/step/pallas_call | solution.py:609
  86.4 2.1 %finish.1 = (bf16[2048,128]{1,0:T(8,128)(2,1)}, f32[2048]{0:T(1024)}) custom-call(bf16[2048,128]{1,0:T(8,128)(2,1)} %step.1.field, bf16[2048,128]{1,0:T(8,128)(2,1)} %fwd.1), custom_call_target="tpu_custom_call" | custom-call | tf_op jit(solution)/shard_map/finish/pallas_call | solution.py:674

commit v6 on v5

--- a/solution.py
+++ b/solution.py
@@ -25,6 +25,7 @@
 P_DEV = NP // N_BOX
 T_DEV = NT // N_DIR
 LAST = P_DEV - 1
+FAR_FIRST = (2, 3, 1, 0)
 SMALL = 11
 
 box_phase = 50.265482
@@ -222,7 +223,7 @@
             src_ref=f.at[pl.ds(pl.multiple_of(b2 * SLOT, SLOT), SLOT), :],
             dst_ref=r.at[pl.ds(pl.multiple_of(b * SLOT, SLOT), SLOT), :],
             send_sem=r_send,
-            recv_sem=r_recv.at[(zh + b2 // N_XY) % 2 * (1 + (b2 // 4 + 8 - b // 4) % 4 // 2)],
+            recv_sem=r_recv.at[(zh + b2 // N_XY) % 2 * (2 - (b2 // 4 + 8 - b // 4) % 4 // 2)],
             device_id=(d, b2),
             device_id_type=MESH,
         )
@@ -494,10 +495,11 @@
         return jnp.dot(gt[...], w[i], preferred_element_type=F32).T.astype(BF)
 
     def send_block(i, carry):
-        at = (1 - zh + i // 4) % 2 * 4 + (b // 4 + i) % 4
+        u = 3 - i % 4
+        at = (1 - zh + i // 4) % 2 * 4 + (b // 4 + u // 2 * 2 + (u // 2 + u % 2) % 2) % 4
         f[pl.ds(pl.multiple_of(at * 256, 256), 256), :] = field_block(at)
-        for j in range(4):
-            b2 = at * 4 + j
+        for j in FAR_FIRST:
+            b2 = at * 4 + (b + j) % 4
 
             @pl.when(b2 != b)
             def _():
@@ -572,7 +574,7 @@
     for piece in range(2):
         lanes = []
         for k in range(2):
-            source = (b // 4 + 4 - 2 * piece - k) % 4
+            source = (b // 4 + 4 - FAR_FIRST[2 * piece + k]) % 4
             lanes.append(pl.ds(pl.multiple_of(there + source * 256, 256), 256))
         wait_for(f.at[:512, :], r_recv.at[1 + piece])
         part = jnp.concatenate([r[k, :] for k in lanes], axis=0)

time: 88.6 us -> 88.8 us (level)
  no operation moved by 1% of the time
where the time goes in v6:
time: 88.8 us; the launch traced here: 87.9 us
  Pallas kernels  87.2 us (98%)
    pallas_call x1, Pallas kernels, step(): pl.pallas_call(step_kernel, out_shape=jax.ShapeDtypeStruct((ROW_DEV, C),...  85.1 us
    pallas_call x1, Pallas kernels, finish(): pl.pallas_call(finish_kernel, out_shape=(jax.ShapeDtypeStruct((ROW_DEV, C...  2.1 us

profile of v6, /device:TPU:32, one launch (start us, length us, event | category | flops | bytes accessed | tf_op | source)
XLA Modules:
  0.0 87.9 jit_solution(18163836794062282480)
XLA Ops:
  0.6 85.1 %step.1.field = bf16[2048,128]{1,0:T(8,128)(2,1)} custom-call(bf16[8,4,256,128]{3,2,1,0:T(8,128)(2,1)} %pat.1, s32[12,64]{1,0:T(8,128)} %bitcast.5, s32[12,128]{1,0:T(8,128)} %bitcast.6, bf16[12,64]{1,0:T(8,128)(2,1)} %bitcast.8, bf16[12,128]{1,0:T(8,128)(2,1)} %bitcast.9, bf16[32,32]{1,0:T(8,128)(2,1)} %constant.13.clone.refs_4_, ...), custom_call_target="tpu_custom_call" | custom-call | tf_op jit(solution)/shard_map/step/pallas_call | solution.py:611
  85.8 2.1 %finish.1 = (bf16[2048,128]{1,0:T(8,128)(2,1)}, f32[2048]{0:T(1024)}) custom-call(bf16[2048,128]{1,0:T(8,128)(2,1)} %step.1.field, bf16[2048,128]{1,0:T(8,128)(2,1)} %fwd.1), custom_call_target="tpu_custom_call" | custom-call | tf_op jit(solution)/shard_map/finish/pallas_call | solution.py:676

commit v7 on v6

--- a/solution.py
+++ b/solution.py
@@ -263,8 +263,13 @@
         each(N_DIR, functools.partial(z_half_copy, zh))
         z_own(LAST, 1).start()
 
+    def far_first(n):
+        u = 3 - n
+        return u // 2 * 2 + (u // 2 + u % 2) % 2
+
     def y_half_copy(half, sem, k):
-        xy2 = (xy + k) % N_XY
+        x2 = (xy // 4 + far_first((k - 1) // 4)) % 4
+        xy2 = x2 * 4 + (xy + far_first((k - 1) % 4)) % 4
         return pltpu.make_async_remote_copy(
             src_ref=ybuf.at[LAST, xy2, half],
             dst_ref=ry.at[LAST, xy, half],

time: 88.8 us -> 89.7 us (1.010)
  Pallas kernels: 87.2 us -> 88.7 us
    pallas_call x1, Pallas kernels: 85.1 us -> 86.6 us  [step(): pl.pallas_call(step_kernel, out_shape=jax.ShapeDtypeStruct((ROW_DEV, C),...]
where the time goes in v7:
time: 89.7 us; the launch traced here: 89.3 us
  Pallas kernels  88.7 us (99%)
    pallas_call x1, Pallas kernels, step(): pl.pallas_call(step_kernel, out_shape=jax.ShapeDtypeStruct((ROW_DEV, C),...  86.6 us
    pallas_call x1, Pallas kernels, finish(): pl.pallas_call(finish_kernel, out_shape=(jax.ShapeDtypeStruct((ROW_DEV, C...  2.1 us

profile of v7, /device:TPU:32, one launch (start us, length us, event | category | flops | bytes accessed | tf_op | source)
XLA Modules:
  0.0 89.3 jit_solution(8307944622610108720)
XLA Ops:
  0.6 86.6 %step.1.field = bf16[2048,128]{1,0:T(8,128)(2,1)} custom-call(bf16[8,4,256,128]{3,2,1,0:T(8,128)(2,1)} %pat.1, s32[12,64]{1,0:T(8,128)} %bitcast.5, s32[12,128]{1,0:T(8,128)} %bitcast.6, bf16[12,64]{1,0:T(8,128)(2,1)} %bitcast.8, bf16[12,128]{1,0:T(8,128)(2,1)} %bitcast.9, bf16[32,32]{1,0:T(8,128)(2,1)} %constant.13.clone.refs_4_, ...), custom_call_target="tpu_custom_call" | custom-call | tf_op jit(solution)/shard_map/step/pallas_call | solution.py:616
  87.2 2.1 %finish.1 = (bf16[2048,128]{1,0:T(8,128)(2,1)}, f32[2048]{0:T(1024)}) custom-call(bf16[2048,128]{1,0:T(8,128)(2,1)} %step.1.field, bf16[2048,128]{1,0:T(8,128)(2,1)} %fwd.1), custom_call_target="tpu_custom_call" | custom-call | tf_op jit(solution)/shard_map/finish/pallas_call | solution.py:681
